TPU v7x, 32 devices: a whole 2x2x4 slice. The times are simulated.
32 devices in a mesh: rows: 16 (over z, x, core), seq: 2 (over y).
Axes of the slice: x: 2, y: 2, z: 4, core: 2. Of those that a mesh axis runs over, the one named last changes fastest.
Arguments:
- tokens: bfloat16 [64, 512, 768], P('rows', 'seq'), may hold values from -6 to 6
- lengths: int32 [64], P('rows'), may hold values from 42 to 512, as said below
- key_mask: int32 [64, 512], P('rows'), may hold values from 0 to 1, as said below
- cotangent: bfloat16 [64, 256, 768], P('rows', 'seq'), may hold values from -6 to 6
- w_qkv: bfloat16 [2, 3, 768, 768], replicated, may hold values from -0.21875 to 0.21875
- w_out: bfloat16 [2, 768, 768], replicated, may hold values from -0.75 to 0.75
- w_pos: bfloat16 [2, 768, 768], replicated, may hold values from -0.21875 to 0.21875
- w_up: bfloat16 [2, 768, 3072], replicated, may hold values from -0.21875 to 0.21875
- w_down: bfloat16 [2, 3072, 768], replicated, may hold values from -0.109375 to 0.109375
- attn_bias: float32 [2, 2, 768], replicated, may hold values from -3 to 3
- up_bias: float32 [2, 3072], replicated, may hold values from -3 to 3
- norm_gain: float32 [2, 2, 768], replicated, may hold values from 0.5 to 1.5
- norm_bias: float32 [2, 2, 768], replicated, may hold values from -2 to 2
- out_bias: float32 [2, 2, 768], replicated, may hold values from -3 to 3
Outputs:
- layer_out: bfloat16 [64, 256, 768], P('rows', 'seq')
- tokens_grad: float32 [64, 512, 768], P('rows', 'seq')
- grad_w_qkv: float32 [2, 3, 768, 768], P(None, None, 'rows')
- grad_w_out: float32 [2, 768, 768], P(None, 'rows')
- grad_w_pos: float32 [2, 768, 768], P(None, 'rows')
- grad_w_up: float32 [2, 768, 3072], P(None, 'rows')
- grad_w_down: float32 [2, 3072, 768], P(None, 'rows')
- grad_attn_bias: float32 [2, 2, 768], P(None, None, 'rows')
- grad_up_bias: float32 [2, 3072], P(None, 'rows')
- grad_norm_gain: float32 [2, 2, 768], P(None, None, 'rows')
- grad_norm_bias: float32 [2, 2, 768], P(None, None, 'rows')
- grad_out_bias: float32 [2, 2, 768], P(None, None, 'rows')
Inputs may be any that keep to these rules, and one draw needn't show every extreme that they name: `lengths`: among the 4 sequences of one index of rows, one has length 512. `key_mask`: position 0 of every sequence is 1.
All inputs are finite; a program needn't handle non-finite values.
Results may differ from a plain program's by a relative error of at most 0.025.
Values may be sent and summed in bfloat16 or wider, within the bound.
A program may use at most 320 MiB of HBM per device.

v0:
```python
import jax
import jax.numpy as jnp
from jax import lax
from jax.sharding import PartitionSpec as P

D = 768
HEADS = 12
HEAD_DIM = 64


epsilon = 1e-06
masked_score = -1000000000.0


def shifted_2(block, axis, distance):
    devices = range(lax.axis_size(axis))
    route = [(i - distance, i) for i in devices if i - distance in devices]
    return lax.ppermute(block, axis, route)


def matmul(left_side, right_side):
    return jnp.dot(left_side, right_side, preferred_element_type=jnp.float32)


def contract(pattern, left_side, right_side):
    return jnp.einsum(pattern, left_side, right_side, preferred_element_type=jnp.float32)


def sinusoid(distance):
    half_width = D // 2
    frequency = 10000.0 ** (-jnp.arange(half_width, dtype=jnp.float32) / half_width)
    angles = distance.astype(jnp.float32)[:, None] * frequency[None, :]
    return jnp.concatenate([jnp.sin(angles), jnp.cos(angles)], axis=1)


def layer_norm(values, scale_gain, shift_bias):
    center = values - jnp.mean(values, axis=-1, keepdims=True)
    variance = jnp.mean(center * center, axis=-1, keepdims=True)
    return center * lax.rsqrt(variance + epsilon) * scale_gain + shift_bias


def norm_back(values, scale_gain, shift_bias, grad_out):
    normed, pullback = jax.vjp(layer_norm, values, scale_gain, shift_bias)
    return pullback(grad_out)


def gelu_tanh(values):
    return jax.nn.gelu(values, approximate=True)


def gelu_back(pre_act, grad_out):
    result, pullback = jax.vjp(gelu_tanh, pre_act)
    return pullback(grad_out)[0]


def rel_shift(relative, stride, key_len):
    seq_sets, head_count, query_len, table_len = relative.shape
    row_width = table_len - stride
    flat_rows = relative.reshape(seq_sets, head_count, query_len * table_len)
    first_cut = stride * (query_len - 1)
    flat_rows = lax.slice_in_dim(flat_rows, first_cut, first_cut + query_len * row_width, axis=2)
    return flat_rows.reshape(seq_sets, head_count, query_len, row_width)[:, :, :, :key_len]


def rel_unshift(grads_in, stride, table_len):
    seq_sets, head_count, query_len, key_len = grads_in.shape
    row_width = table_len - stride
    padded = jnp.pad(grads_in, ((0, 0), (0, 0), (0, 0), (0, row_width - key_len)))
    flat_rows = padded.reshape(seq_sets, head_count, query_len * row_width)
    flat_rows = jnp.pad(flat_rows, ((0, 0), (0, 0), (stride * (query_len - 1), stride)))
    return flat_rows.reshape(seq_sets, head_count, query_len, table_len)


def attention_scores(query_w, query_r, keys_all, pos_table, stride, key_valid):
    seq_sets, query_len = (query_w.shape[0], query_w.shape[1])
    key_len = keys_all.shape[1]
    head_q = query_w.reshape(seq_sets, query_len, HEADS, HEAD_DIM)
    head_r = query_r.reshape(seq_sets, query_len, HEADS, HEAD_DIM)
    head_k = keys_all.reshape(seq_sets, key_len, HEADS, HEAD_DIM)
    table_heads = pos_table.reshape(pos_table.shape[0], HEADS, HEAD_DIM)
    content = contract("sphc,sjhc->shpj", head_q, head_k)
    relative = contract("sphc,rhc->shpr", head_r, table_heads)
    position = rel_shift(relative, stride, key_len)
    scores = (content + position) * HEAD_DIM ** (-0.5)
    return jnp.where(key_valid[:, None, None, :] > 0, scores, masked_score)


def layer_forward(
    residual,
    query_in,
    key_in,
    key_valid,
    first_row,
    stride,
    dist_unit,
    params,
    layer_id,
    gather_pair,
):
    w_qkv, w_out, w_pos, w_up, w_down, attn_bias, up_bias, norm_gain, norm_bias, out_bias = params
    seq_sets, query_len, model_width = query_in.shape
    queries = matmul(query_in, w_qkv[layer_id, 0])
    keys_part = matmul(key_in, w_qkv[layer_id, 1]).astype(jnp.bfloat16)
    values_part = matmul(key_in, w_qkv[layer_id, 2]).astype(jnp.bfloat16)
    keys_all, values_all = gather_pair(keys_part, values_part)
    key_len = keys_all.shape[1]
    query_w = (queries + attn_bias[layer_id, 0]).astype(jnp.bfloat16)
    query_r = (queries + attn_bias[layer_id, 1]).astype(jnp.bfloat16)
    table_len = stride * (query_len - 1) + key_len
    top_dist = stride * (first_row + query_len - 1)
    distance = (top_dist - jnp.arange(table_len, dtype=jnp.int32)) * dist_unit
    encoding = sinusoid(distance).astype(jnp.bfloat16)
    pos_table = matmul(encoding, w_pos[layer_id]).astype(jnp.bfloat16)
    scores = attention_scores(query_w, query_r, keys_all, pos_table, stride, key_valid)
    top_score = jnp.max(scores, axis=-1, keepdims=True)
    exp_terms = jnp.exp(scores - top_score)
    totals = jnp.sum(exp_terms, axis=-1, keepdims=True)
    log_total = top_score + jnp.log(totals)
    attn_prob = (exp_terms / totals).astype(jnp.bfloat16)
    head_v = values_all.reshape(seq_sets, key_len, HEADS, HEAD_DIM)
    mixed_heads = contract("shpj,sjhc->sphc", attn_prob, head_v).reshape(
        seq_sets, query_len, model_width
    )
    mixed_low = mixed_heads.astype(jnp.bfloat16)
    pre_norm = residual + (matmul(mixed_low, w_out[layer_id]) + out_bias[layer_id, 0])
    hidden = layer_norm(pre_norm, norm_gain[layer_id, 0], norm_bias[layer_id, 0])
    hidden_low = hidden.astype(jnp.bfloat16)
    pre_act = matmul(hidden_low, w_up[layer_id]) + up_bias[layer_id]
    act_low = gelu_tanh(pre_act).astype(jnp.bfloat16)
    post_norm = hidden + (matmul(act_low, w_down[layer_id]) + out_bias[layer_id, 1])
    output = layer_norm(post_norm, norm_gain[layer_id, 1], norm_bias[layer_id, 1])
    saved_state = (
        query_in,
        key_in,
        key_valid,
        keys_all,
        values_all,
        query_w,
        query_r,
        encoding,
        pos_table,
        log_total,
        mixed_low,
        pre_norm,
        hidden_low,
        pre_act,
        act_low,
        post_norm,
    )
    return (output, saved_state)


def layer_backward(grad_out, saved_state, stride, params, layer_id, scatter_pair):
    w_qkv, w_out, w_pos, w_up, w_down, attn_bias, up_bias, norm_gain, norm_bias, out_bias = params
    (
        query_in,
        key_in,
        key_valid,
        keys_all,
        values_all,
        query_w,
        query_r,
        encoding,
        pos_table,
        log_total,
        mixed_low,
        pre_norm,
        hidden_low,
        pre_act,
        act_low,
        post_norm,
    ) = saved_state
    seq_sets, query_len, model_width = query_in.shape
    key_len = keys_all.shape[1]
    table_len = pos_table.shape[0]
    score_scale = HEAD_DIM ** (-0.5)
    d_post, d_gain_two, d_bias_two = norm_back(
        post_norm, norm_gain[layer_id, 1], norm_bias[layer_id, 1], grad_out
    )
    d_ffn = d_post.astype(jnp.bfloat16)
    d_down = contract("spf,spd->fd", act_low, d_ffn)
    d_act = contract("spd,fd->spf", d_ffn, w_down[layer_id])
    d_pre = gelu_back(pre_act, d_act).astype(jnp.bfloat16)
    d_up = contract("spd,spf->df", hidden_low, d_pre)
    d_hidden = d_post + contract("spf,df->spd", d_pre, w_up[layer_id])
    d_pre_norm, d_gain_one, d_bias_one = norm_back(
        pre_norm, norm_gain[layer_id, 0], norm_bias[layer_id, 0], d_hidden
    )
    d_branch = d_pre_norm.astype(jnp.bfloat16)
    d_wout = contract("spe,spd->ed", mixed_low, d_branch)
    d_mixed = contract("spd,ed->spe", d_branch, w_out[layer_id]).astype(jnp.bfloat16)
    scores = attention_scores(query_w, query_r, keys_all, pos_table, stride, key_valid)
    prob_full = jnp.exp(scores - log_total)
    attn_prob = prob_full.astype(jnp.bfloat16)
    head_q = query_w.reshape(seq_sets, query_len, HEADS, HEAD_DIM)
    head_r = query_r.reshape(seq_sets, query_len, HEADS, HEAD_DIM)
    head_k = keys_all.reshape(seq_sets, key_len, HEADS, HEAD_DIM)
    head_v = values_all.reshape(seq_sets, key_len, HEADS, HEAD_DIM)
    head_dm = d_mixed.reshape(seq_sets, query_len, HEADS, HEAD_DIM)
    table_heads = pos_table.reshape(table_len, HEADS, HEAD_DIM)
    d_prob = contract("sphc,sjhc->shpj", head_dm, head_v)
    d_values = contract("shpj,sphc->sjhc", attn_prob, head_dm)
    row_inner = jnp.sum(d_prob * prob_full, axis=-1, keepdims=True)
    d_scores = (prob_full * (d_prob - row_inner)).astype(jnp.bfloat16)
    d_query_w = (contract("shpj,sjhc->sphc", d_scores, head_k) * score_scale).reshape(
        seq_sets, query_len, model_width
    )
    d_keys = contract("shpj,sphc->sjhc", d_scores, head_q) * score_scale
    d_relative = rel_unshift(d_scores, stride, table_len)
    d_query_r = (contract("shpr,rhc->sphc", d_relative, table_heads) * score_scale).reshape(
        seq_sets, query_len, model_width
    )
    d_table = contract("shpr,sphc->rhc", d_relative, head_r) * score_scale
    d_wpos = jnp.einsum(
        "re,rd->ed",
        encoding.astype(jnp.float32),
        d_table.reshape(table_len, model_width),
        precision=lax.Precision.HIGHEST,
    )
    d_queries = (d_query_w + d_query_r).astype(jnp.bfloat16)
    d_attn = jnp.stack([jnp.sum(d_query_w, axis=(0, 1)), jnp.sum(d_query_r, axis=(0, 1))])
    d_keys_sum, d_values_sum = scatter_pair(
        d_keys.reshape(seq_sets, key_len, model_width),
        d_values.reshape(seq_sets, key_len, model_width),
    )
    d_keys_low = d_keys_sum.astype(jnp.bfloat16)
    d_values_low = d_values_sum.astype(jnp.bfloat16)
    d_wq = contract("spe,spd->ed", query_in, d_queries)
    d_wk = contract("spe,spd->ed", key_in, d_keys_low)
    d_wv = contract("spe,spd->ed", key_in, d_values_low)
    d_query_in = contract("spd,ed->spe", d_queries, w_qkv[layer_id, 0])
    d_key_in = contract("spd,ed->spe", d_keys_low, w_qkv[layer_id, 1]) + contract(
        "spd,ed->spe", d_values_low, w_qkv[layer_id, 2]
    )
    weight_grads = (
        jnp.stack([d_wq, d_wk, d_wv]),
        d_wout,
        d_wpos,
        d_up,
        d_down,
        d_attn,
        jnp.sum(d_pre.astype(jnp.float32), axis=(0, 1)),
        jnp.stack([d_gain_one, d_gain_two]),
        jnp.stack([d_bias_one, d_bias_two]),
        jnp.stack(
            [
                jnp.sum(d_branch.astype(jnp.float32), axis=(0, 1)),
                jnp.sum(d_ffn.astype(jnp.float32), axis=(0, 1)),
            ]
        ),
    )
    return (d_pre_norm, d_query_in, d_key_in, weight_grads)


def split_rim(edge_rows):
    return shifted_2(edge_rows, "seq", 1)


def split_rim_back(edge_grads):
    return shifted_2(edge_grads, "seq", -1)


def split_gather_one(keys_part, values_part):
    return (
        lax.all_gather(keys_part, "seq", axis=1, tiled=True),
        lax.all_gather(values_part, "seq", axis=1, tiled=True),
    )


def split_gather_two(keys_part, values_part):
    return (
        lax.all_gather(keys_part, "seq", axis=1, tiled=True),
        lax.all_gather(values_part, "seq", axis=1, tiled=True),
    )


def split_scatter_one(keys_grad, values_grad):
    return (
        lax.psum_scatter(
            keys_grad.astype(jnp.bfloat16), "seq", scatter_dimension=1, tiled=True
        ).astype(jnp.float32),
        lax.psum_scatter(
            values_grad.astype(jnp.bfloat16), "seq", scatter_dimension=1, tiled=True
        ).astype(jnp.float32),
    )


def split_scatter_two(keys_grad, values_grad):
    return (
        lax.psum_scatter(
            keys_grad.astype(jnp.bfloat16), "seq", scatter_dimension=1, tiled=True
        ).astype(jnp.float32),
        lax.psum_scatter(
            values_grad.astype(jnp.bfloat16), "seq", scatter_dimension=1, tiled=True
        ).astype(jnp.float32),
    )


def train_step(tokens, lengths, key_mask, cotangent, params, seq_index, link_set):
    rim_in, rim_back, gather_one, gather_two, scatter_one, scatter_two = link_set
    seq_sets, local_len, model_width = tokens.shape
    full_len = key_mask.shape[1]
    places = jnp.arange(full_len, dtype=jnp.int32)[None, :]
    key_valid = jnp.where(places < lengths[:, None], key_mask, 0)
    shifted_valid = jnp.concatenate([key_valid[:, :1], key_valid[:, :-1]], axis=1)
    pooled_valid = jnp.max(shifted_valid.reshape(seq_sets, full_len // 2, 2), axis=2)
    edge_rows = rim_in(tokens[:, -1:, :])
    previous = jnp.where(seq_index == 0, tokens[:, :1, :], edge_rows)
    shifted = jnp.concatenate([previous, tokens[:, :-1, :]], axis=1).astype(jnp.float32)
    pooled = jnp.mean(shifted.reshape(seq_sets, local_len // 2, 2, model_width), axis=2)
    pooled_low = pooled.astype(jnp.bfloat16)
    first_row = seq_index * (local_len // 2)
    first_out, saved_first = layer_forward(
        pooled, pooled_low, tokens, key_valid, first_row, 2, 1, params, 0, gather_one
    )
    first_low = first_out.astype(jnp.bfloat16)
    second, saved_second = layer_forward(
        first_out, first_low, first_low, pooled_valid, first_row, 1, 2, params, 1, gather_two
    )
    d_first, d_query_two, d_key_two, grads_two = layer_backward(
        cotangent.astype(jnp.float32), saved_second, 1, params, 1, scatter_two
    )
    d_first = d_first + (d_query_two + d_key_two)
    recomputed, state_one = layer_forward(
        pooled, pooled_low, tokens, key_valid, first_row, 2, 1, params, 0, gather_one
    )
    d_pooled, d_query_one, d_key_one, grads_one = layer_backward(
        d_first, state_one, 2, params, 0, scatter_one
    )
    d_shifted = jnp.repeat((d_pooled + d_query_one) * 0.5, 2, axis=1)
    incoming = rim_back(d_shifted[:, :1, :])
    own_first = jnp.where(seq_index == 0, d_shifted[:, :1, :], jnp.zeros_like(incoming))
    d_tokens = d_key_one + jnp.concatenate([d_shifted[:, 1:, :], incoming], axis=1)
    d_tokens = d_tokens + jnp.concatenate([own_first, jnp.zeros_like(d_tokens[:, 1:, :])], axis=1)
    weight_grads = tuple(
        (jnp.stack([one_item, two_item]) for one_item, two_item in zip(grads_one, grads_two))
    )
    return (second.astype(jnp.bfloat16), d_tokens, weight_grads)


def on_device(
    tokens,
    lengths,
    key_mask,
    cotangent,
    w_qkv,
    w_out,
    w_pos,
    w_up,
    w_down,
    attn_bias,
    up_bias,
    norm_gain,
    norm_bias,
    out_bias,
):
    params = (w_qkv, w_out, w_pos, w_up, w_down, attn_bias, up_bias, norm_gain, norm_bias, out_bias)
    link_set = (
        split_rim,
        split_rim_back,
        split_gather_one,
        split_gather_two,
        split_scatter_one,
        split_scatter_two,
    )
    layer_out, tokens_grad, weight_grads = train_step(
        tokens, lengths, key_mask, cotangent, params, lax.axis_index("seq"), link_set
    )
    (
        grad_qkv,
        grad_out,
        grad_pos,
        grad_up,
        grad_down,
        grad_attn,
        grad_upb,
        grad_gain,
        grad_nbias,
        grad_obias,
    ) = weight_grads
    grad_qkv = grad_qkv.reshape(6, D, D)
    grad_attn = grad_attn.reshape(4, D)
    grad_gain = grad_gain.reshape(4, D)
    grad_nbias = grad_nbias.reshape(4, D)
    grad_obias = grad_obias.reshape(4, D)
    (
        sum_qkv,
        sum_out,
        sum_pos,
        sum_up,
        sum_down,
        sum_attn,
        sum_upb,
        sum_gain,
        sum_nbias,
        sum_obias,
    ) = (
        lax.psum_scatter(grad_qkv, ("rows", "seq"), scatter_dimension=1, tiled=True),
        lax.psum_scatter(grad_out, ("rows", "seq"), scatter_dimension=1, tiled=True),
        lax.psum_scatter(grad_pos, ("rows", "seq"), scatter_dimension=1, tiled=True),
        lax.psum_scatter(grad_up, ("rows", "seq"), scatter_dimension=1, tiled=True),
        lax.psum_scatter(grad_down, ("rows", "seq"), scatter_dimension=1, tiled=True),
        lax.psum_scatter(grad_attn, ("rows", "seq"), scatter_dimension=1, tiled=True),
        lax.psum_scatter(grad_upb, ("rows", "seq"), scatter_dimension=1, tiled=True),
        lax.psum_scatter(grad_gain, ("rows", "seq"), scatter_dimension=1, tiled=True),
        lax.psum_scatter(grad_nbias, ("rows", "seq"), scatter_dimension=1, tiled=True),
        lax.psum_scatter(grad_obias, ("rows", "seq"), scatter_dimension=1, tiled=True),
    )
    totals = (
        lax.all_gather(sum_qkv.astype(jnp.bfloat16), "seq", axis=1, tiled=True).astype(
            sum_qkv.dtype
        ),
        lax.all_gather(sum_out.astype(jnp.bfloat16), "seq", axis=1, tiled=True).astype(
            sum_out.dtype
        ),
        lax.all_gather(sum_pos.astype(jnp.bfloat16), "seq", axis=1, tiled=True).astype(
            sum_pos.dtype
        ),
        lax.all_gather(sum_up.astype(jnp.bfloat16), "seq", axis=1, tiled=True).astype(sum_up.dtype),
        lax.all_gather(sum_down.astype(jnp.bfloat16), "seq", axis=1, tiled=True).astype(
            sum_down.dtype
        ),
        lax.all_gather(sum_attn.astype(jnp.bfloat16), "seq", axis=1, tiled=True).astype(
            sum_attn.dtype
        ),
        lax.all_gather(sum_upb.astype(jnp.bfloat16), "seq", axis=1, tiled=True).astype(
            sum_upb.dtype
        ),
        lax.all_gather(sum_gain.astype(jnp.bfloat16), "seq", axis=1, tiled=True).astype(
            sum_gain.dtype
        ),
        lax.all_gather(sum_nbias.astype(jnp.bfloat16), "seq", axis=1, tiled=True).astype(
            sum_nbias.dtype
        ),
        lax.all_gather(sum_obias.astype(jnp.bfloat16), "seq", axis=1, tiled=True).astype(
            sum_obias.dtype
        ),
    )
    return (
        layer_out,
        tokens_grad,
        totals[0].reshape(2, 3, -1, D),
        totals[1],
        totals[2],
        totals[3],
        totals[4],
        totals[5].reshape(2, 2, -1),
        totals[6],
        totals[7].reshape(2, 2, -1),
        totals[8].reshape(2, 2, -1),
        totals[9].reshape(2, 2, -1),
    )


def solution(mesh):
    in_specs = (
        P("rows", "seq", None),
        P("rows"),
        P("rows", None),
        P("rows", "seq", None),
        P(),
        P(),
        P(),
        P(),
        P(),
        P(),
        P(),
        P(),
        P(),
        P(),
    )
    out_specs = (
        P("rows", "seq", None),
        P("rows", "seq", None),
        P(None, None, "rows", None),
        P(None, "rows", None),
        P(None, "rows", None),
        P(None, "rows", None),
        P(None, "rows", None),
        P(None, None, "rows"),
        P(None, "rows"),
        P(None, None, "rows"),
        P(None, None, "rows"),
        P(None, None, "rows"),
    )
    return jax.shard_map(
        on_device, mesh=mesh, in_specs=in_specs, out_specs=out_specs, check_vma=False
    )
```

profile of v0, /device:TPU:0, one launch (start us, length us, event | category | flops | bytes accessed | tf_op | source)
XLA Modules:
  0.0 1448.1 jit_solution(14761127993948067921)
XLA Ops:
  61.4 18.9 %copy.230 = f32[4,12,128,766]{3,2,0,1:T(8,128)} copy(f32[4,12,128,766]{2,3,0,1:T(8,128)} %convolution_bitcast_fusion) | data formatting | bytes 37650432 | tf_op jit(solution)/shard_map/sphc,rhc->shpr/transpose | solution.py:26
  80.3 24.0 %reshape.392 = f32[4,12,98048]{2,0,1:T(4,128)} reshape(f32[4,12,128,766]{3,2,0,1:T(8,128)} %copy.230) | data formatting | bytes 37650432 | tf_op jit(solution)/shard_map/reshape | solution.py:59
  104.3 20.2 %slice.209 = f32[4,12,97792]{2,0,1:T(4,128)} slice(f32[4,12,98048]{2,0,1:T(4,128)} %reshape.392), slice={[0:4], [0:12], [254:98046]} | slice | bytes 37552128 | tf_op jit(solution)/shard_map/slice | solution.py:61
  124.5 27.6 %reshape.393 = f32[4,12,128,764]{3,2,0,1:T(8,128)} reshape(f32[4,12,97792]{2,0,1:T(4,128)} %slice.209) | data formatting | bytes 37552128 | tf_op jit(solution)/shard_map/reshape | solution.py:62
  220.7 9.8 copy.241
  230.4 15.7 %reshape.400 = f32[4,12,49024]{2,0,1:T(4,128)} reshape(f32[4,12,128,383]{3,2,0,1:T(8,128)} %copy.241) | data formatting | bytes 18825216 | tf_op jit(solution)/shard_map/reshape | solution.py:59
  246.1 12.1 slice.213
  258.2 16.3 %reshape.401 = f32[4,12,128,382]{3,2,0,1:T(8,128)} reshape(f32[4,12,48896]{2,0,1:T(4,128)} %slice.213) | data formatting | bytes 18776064 | tf_op jit(solution)/shard_map/reshape | solution.py:62
  306.8 8.9 convert_reduce_fusion
  348.3 12.4 reshape.403
  368.2 14.0 reshape.404
  402.3 9.6 convert_reduce_fusion.1
  476.1 19.0 %reshape.406 = bf16[4,12,97792]{2,0,1:T(4,128)(2,1)} reshape(bf16[4,12,128,764]{3,2,0,1:T(8,128)(2,1)} %pad.19.clone) | data formatting | bytes 18776064 | tf_op jit(solution)/shard_map/reshape | solution.py:69
  495.1 9.4 pad.20
  504.5 23.1 %reshape.407 = bf16[4,12,128,766]{3,2,0,1:T(8,128)(2,1)} reshape(bf16[4,12,98048]{2,0,1:T(4,128)(2,1)} %pad.20) | data formatting | bytes 18825216 | tf_op jit(solution)/shard_map/reshape | solution.py:71
  603.7 11.9 pad_maximum_fusion.2
  617.1 40.1 %all-reduce.9 = (bf16[4,768]{1,0:T(4,128)(2,1)S(1)}, bf16[4,768]{1,0:T(4,128)(2,1)S(1)}, bf16[4,768]{1,0:T(4,128)(2,1)S(1)}, bf16[4,768]{1,0:T(4,128)(2,1)S(1)}) all-reduce(f32[4,768]{1,0:T(4,128)S(1)} %reshape.414, f32[4,768]{1,0:T(4,128)S(1)} %reshape.417, ...), channel_id=11, replica_groups=mesh['rows'=16,'seq'=2] {'rows','seq'}, use_global_device_ids=true, to_apply=%region_37.38.clone | all-reduce | flops 12288 | bytes 73728
  696.1 35.8 %reduce-scatter.27.cloned.1.call-done = f32[2,24,768]{2,1,0:T(8,128)} async-done(((f32[2,768,768]{2,1,0:T(8,128)}), f32[2,24,768]{2,1,0:T(8,128)}) %reduce-scatter.27.cloned.1.call-update) | async-done | bytes 147472 | tf_op jit(solution)/shard_map/reduce_scatter | solution.py:399
  732.8 111.6 %reduce-scatter.29.cloned.1.call-done = f32[2,24,768]{2,1,0:T(8,128)} async-done(((f32[2,768,768]{2,1,0:T(8,128)}), f32[2,24,768]{2,1,0:T(8,128)}) %reduce-scatter.29.cloned.1.call-update) | async-done | bytes 147472 | tf_op jit(solution)/shard_map/reduce_scatter | solution.py:400
  864.8 190.0 %reduce-scatter.33.cloned.1.call-done = f32[2,96,768]{2,1,0:T(8,128)} async-done(((f32[2,3072,768]{2,1,0:T(8,128)}), f32[2,96,768]{2,1,0:T(8,128)}) %reduce-scatter.33.cloned.1.call-update) | async-done | bytes 589840 | tf_op jit(solution)/shard_map/reduce_scatter | solution.py:402
  1055.9 8.2 all_gather.52
  1065.2 199.9 %reduce-scatter.31.cloned.1.call-done = f32[2,24,3072]{2,1,0:T(8,128)} async-done(((f32[2,768,3072]{2,1,0:T(8,128)}), f32[2,24,3072]{2,1,0:T(8,128)}) %reduce-scatter.31.cloned.1.call-update) | async-done | bytes 589840 | tf_op jit(solution)/shard_map/reduce_scatter | solution.py:401
  1266.3 8.2 all_gather.51
  1275.6 157.1 %reduce-scatter.25.cloned.1.call-done = f32[6,24,768]{2,1,0:T(8,128)} async-done(((f32[6,768,768]{2,1,0:T(8,128)}), f32[6,24,768]{2,1,0:T(8,128)}) %reduce-scatter.25.cloned.1.call-update) | async-done | bytes 442384 | tf_op jit(solution)/shard_map/reduce_scatter | solution.py:398
  (548 shorter events, 427.6 us)
Async XLA Ops:
  7.2 144.9 %all-gather.12.cloned.1.call-start = ((), (), s32[]{:S(2)}) async-start(), calls=%async_computation.11 | async-start | bytes 4718592 | tf_op jit(solution)/shard_map/all_gather | solution.py:265
  11.7 159.5 %all-gather.10.cloned.1.call-start = ((), (), s32[]{:S(2)}) async-start(), calls=%async_computation.10 | async-start | bytes 4718592 | tf_op jit(solution)/shard_map/all_gather | solution.py:266
  11.8 22.7 %collective-permute-start = (bf16[4,1,768]{2,1,0:T(2,128)(2,1)S(1)}, bf16[4,1,768]{2,1,0:T(2,128)(2,1)S(1)}, u32[]{:S(2)}, u32[]{:S(2)}) collective-permute-start(bf16[4,1,768]{2,1,0:T(2,128)(2,1)S(1)} %slice.167), channel_id=1, source_target_pairs={{0,1},{2,3},{4,5},{6,7},{8,9},{10,11},{12,13},{14,15},{16,17},{18,... | collective-permute-start | bytes 18440 | tf_op jit(solution)/shard_map/ppermute | solution.py:18
  20.8 253.7 %all-gather.16.cloned.1.call-start = ((), (), s32[]{:S(2)}) async-start(), calls=%async_computation.13 | async-start | bytes 2359296 | tf_op jit(solution)/shard_map/all_gather | solution.py:272
  34.5 19.0 %copy-start.9 = (bf16[766,768]{0,1:T(8,128)(2,1)}, bf16[766,768]{0,1:T(8,128)(2,1)S(1)}, u32[]{:S(2)}) copy-start(bf16[766,768]{0,1:T(8,128)(2,1)S(1)} %copy.227) | copy-start | bytes 3529732
  193.0 97.4 %copy-start.3 = (f32[4,128,768]{2,1,0:T(8,128)}, f32[4,128,768]{2,1,0:T(8,128)S(1)}, u32[]{:S(2)}) copy-start(f32[4,128,768]{2,1,0:T(8,128)S(1)} %get-tuple-element.88) | copy-start | bytes 4718596
  197.8 86.7 %all-gather.14.cloned.1.call-start = ((), (), s32[]{:S(2)}) async-start(), calls=%async_computation.12 | async-start | bytes 2359296 | tf_op jit(solution)/shard_map/all_gather | solution.py:273
  208.5 184.2 %reduce-scatter.17.cloned.1.call-start = ((), (), s32[]{:S(2)}) async-start(), calls=%async_computation.14 | async-start | bytes 2359296 | tf_op jit(solution)/shard_map/reduce_scatter | solution.py:290
  291.6 28.1 %copy-start.17 = (f32[4,128,768]{2,1,0:T(8,128)}, f32[4,128,768]{2,1,0:T(8,128)S(1)}, u32[]{:S(2)}) copy-start(f32[4,128,768]{2,1,0:T(8,128)S(1)} %get-tuple-element.92) | copy-start | bytes 4718596
  291.6 28.1 %copy-start.76 = (f32[4,128]{1,0:T(4,128)}, f32[4,128]{1,0:T(4,128)S(1)}, u32[]{:S(2)}) copy-start(f32[4,128]{1,0:T(4,128)S(1)} %broadcast_multiply_fusion.1) | copy-start | bytes 6148
  291.9 27.8 %copy-start.107 = (f32[4,128]{1,0:T(4,128)}, f32[4,128]{1,0:T(4,128)S(1)}, u32[]{:S(2)}) copy-start(f32[4,128]{1,0:T(4,128)S(1)} %fusion.157) | copy-start | bytes 6148
  336.8 59.5 %reduce-scatter.19.cloned.1.call-start = ((), (), s32[]{:S(2)}) async-start(), calls=%async_computation.15 | async-start | bytes 2359296 | tf_op jit(solution)/shard_map/reduce_scatter | solution.py:293
  345.2 246.9 %reduce-scatter.23.cloned.1.call-start = ((), (), s32[]{:S(2)}) async-start(), calls=%async_computation.17 | async-start | bytes 4718592 | tf_op jit(solution)/shard_map/reduce_scatter | solution.py:282
  428.1 168.8 %reduce-scatter.21.cloned.1.call-start = ((), (), s32[]{:S(2)}) async-start(), calls=%async_computation.16 | async-start | bytes 4718592 | tf_op jit(solution)/shard_map/reduce_scatter | solution.py:279
  447.4 242.4 %reduce-scatter.35.cloned.1.call-start = ((), (), s32[]{:S(2)}) async-start(), calls=%async_computation.23 | async-start | bytes 1622016
  455.8 276.1 %reduce-scatter.27.cloned.1.call-start = ((), (), s32[]{:S(2)}) async-start(), calls=%async_computation.19 | async-start | bytes 4866048 | tf_op jit(solution)/shard_map/reduce_scatter | solution.py:399
  460.0 384.4 %reduce-scatter.29.cloned.1.call-start = ((), (), s32[]{:S(2)}) async-start(), calls=%async_computation.20 | async-start | bytes 4866048 | tf_op jit(solution)/shard_map/reduce_scatter | solution.py:400
  504.5 23.1 %copy-start.26 = (bf16[4,128,768]{1,2,0:T(8,128)(2,1)S(1)}, bf16[4,128,768]{1,2,0:T(8,128)(2,1)}, u32[]{:S(2)}) copy-start(bf16[4,128,768]{1,2,0:T(8,128)(2,1)} %copy-done.25) | copy-start | bytes 2359300
  538.6 516.2 %reduce-scatter.33.cloned.1.call-start = ((), (), s32[]{:S(2)}) async-start(), calls=%async_computation.22 | async-start | bytes 19464192 | tf_op jit(solution)/shard_map/reduce_scatter | solution.py:402
  558.7 706.5 %reduce-scatter.31.cloned.1.call-start = ((), (), s32[]{:S(2)}) async-start(), calls=%async_computation.21 | async-start | bytes 19464192 | tf_op jit(solution)/shard_map/reduce_scatter | solution.py:401
  575.0 857.7 %reduce-scatter.25.cloned.1.call-start = ((), (), s32[]{:S(2)}) async-start(), calls=%async_computation.18 | async-start | bytes 14598144 | tf_op jit(solution)/shard_map/reduce_scatter | solution.py:398
  615.7 61.9 %copy-start.36 = (f32[4,128,768]{2,1,0:T(8,128)S(1)}, f32[4,128,768]{2,1,0:T(8,128)}, u32[]{:S(2)}) copy-start(f32[4,128,768]{2,1,0:T(8,128)} %copy-done.35) | copy-start | bytes 4718596
  615.7 61.9 %copy-start.111 = (f32[4,128]{1,0:T(4,128)S(1)}, f32[4,128]{1,0:T(4,128)}, u32[]{:S(2)}) copy-start(f32[4,128]{1,0:T(4,128)} %copy-done.110) | copy-start | bytes 6148
  688.5 171.8 %collective-permute-start.1 = (f32[4,1,768]{2,1,0:T(1,128)S(1)}, f32[4,1,768]{2,1,0:T(1,128)S(1)}, u32[]{:S(2)}, u32[]{:S(2)}) collective-permute-start(f32[4,1,768]{2,1,0:T(1,128)S(1)} %get-tuple-element.63), channel_id=1, source_target_pairs={{1,0},{3,2},{5,4},{7,6},{9,8},{11,10},{13,12},{15,14},{17,16},{19,... | collective-permute-start | bytes 36872 | tf_op jit(solution)/shard_map/ppermute | solution.py:18
  (139 other events, 635.6 us)
Sparse Core Ops, SparseCore 0:
  11.8 47.6 all-gather.11
  61.0 44.9 all-gather.9
  197.9 27.4 all-gather.15
  227.4 27.2 all-gather.13
  336.9 26.3 reduce-scatter.16
  365.5 26.0 reduce-scatter.18
  428.2 43.6 reduce-scatter.22
  474.8 43.3 reduce-scatter.20
  523.4 97.0 reduce-scatter.34
  625.8 106.0 reduce-scatter.26
  738.3 106.0 reduce-scatter.28
  850.7 204.0 reduce-scatter.32
  1061.2 203.9 reduce-scatter.30
  1271.0 161.6 reduce-scatter.24
where the time goes:
time: 1460 us; the launch traced here: 1450 us
  waiting for transfers between devices  695 us (48%)
  local copies, waits for them, and re-layouts  310 us (21%)
  matrix products  233 us (16%)
  blocking collectives  95.5 us (7%)
  other arithmetic  90.1 us (6%)
  between operations  16.7 us (1%)
    reduce_scatter x1, waiting for transfers between devices, on_device(): lax.psum_scatter(grad_up, ('rows', 'seq'), scatter_dimension=1, tiled=True)  200 us
    reduce_scatter x1, waiting for transfers between devices, on_device(): lax.psum_scatter(grad_down, ('rows', 'seq'), scatter_dimension=1, tiled=T...  190 us
    dot_general x42, matrix products, contract(): jnp.einsum(pattern, left_side, right_side, preferred_element_type=jnp.flo...  177 us
    reduce_scatter x1, waiting for transfers between devices, on_device(): lax.psum_scatter(grad_qkv, ('rows', 'seq'), scatter_dimension=1, tiled=True)  157 us
    reduce_scatter x1, waiting for transfers between devices, on_device(): lax.psum_scatter(grad_pos, ('rows', 'seq'), scatter_dimension=1, tiled=True)  112 us
    dot_general x14, matrix products, matmul(): return jnp.dot(left_side, right_side, preferred_element_type=jnp.float32)  48.4 us
    reshape x2, local copies, waits for them, and re-layouts, rel_shift(): flat_rows.reshape(seq_sets, head_count, query_len, row_width)  43.9 us
    unnamed x1, blocking collectives  40.1 us
  transfers between devices with their start and end apart: 16, of which 5 were waited for; matrix products, arithmetic and copies ran while one was open for 35% of the time, Pallas kernels for 0%

commit v1 on v0

v1 whole, which is shorter than its diff:
```python
import functools

import jax
import jax.numpy as jnp
from jax import lax
from jax.experimental import pallas as pl
from jax.experimental.pallas import tpu as pltpu
from jax.sharding import PartitionSpec as P

D = 768
HEADS = 12
HEAD_DIM = 64
FF = 3072
PANELS = FF // D
HALF = D // 2
EPS = 1e-06
MASKED = -1000000000.0
SCALE = HEAD_DIM ** (-0.5)
BF = jnp.bfloat16
F32 = jnp.float32
MIB = 1 << 20

SHARDS = 16
UP_ROWS = PANELS * D // SHARDS
ROW = D // SHARDS


def mm(a, b):
    return lax.dot_general(a, b, (((1,), (0,)), ((), ())), preferred_element_type=F32)


def mm_nt(a, b):
    return lax.dot_general(a, b, (((1,), (1,)), ((), ())), preferred_element_type=F32)


def mm_tn(a, b):
    return lax.dot_general(a, b, (((0,), (0,)), ((), ())), preferred_element_type=F32)


def ln_fwd(z):
    center = z - jnp.mean(z, axis=-1, keepdims=True)
    var = jnp.mean(center * center, axis=-1, keepdims=True)
    rstd = lax.rsqrt(var + EPS)
    return center * rstd, rstd


def ln_bwd(dy, xhat, rstd, gain):
    dx = dy * gain
    m1 = jnp.mean(dx, axis=-1, keepdims=True)
    m2 = jnp.mean(dx * xhat, axis=-1, keepdims=True)
    return rstd * (dx - m1 - xhat * m2)


GELU_K = 0.7978845608028654
GELU_C = 0.044715


def gelu_and_slope(z):
    z2 = z * z
    t = jnp.tanh(GELU_K * z * (1.0 + GELU_C * z2))
    half = 0.5 * (1.0 + t)
    slope = half + 0.5 * z * (1.0 - t * t) * (GELU_K * (1.0 + 3.0 * GELU_C * z2))
    return z * half, slope


def split_hi_lo(x):
    hi = x.astype(BF)
    return hi, (x - hi.astype(F32)).astype(BF)


def cost(flops, nbytes, trans=0):
    return pl.CostEstimate(flops=int(flops), bytes_accessed=int(nbytes), transcendentals=int(trans))


def params(limit=56, **kw):
    return pltpu.CompilerParams(vmem_limit_bytes=limit * MIB, **kw)


def full_spec(shape, memory_space=pltpu.VMEM):
    return pl.BlockSpec(memory_space=memory_space)


ANY = pl.BlockSpec(memory_space=pl.ANY)
VM = pl.BlockSpec(memory_space=pltpu.VMEM)
SM = pl.BlockSpec(memory_space=pltpu.SMEM)


def sds(shape, dtype):
    return jax.ShapeDtypeStruct(shape, dtype)


def pool_matrix(rows, cols):
    k = lax.broadcasted_iota(jnp.int32, (rows, cols), 0)
    t = lax.broadcasted_iota(jnp.int32, (rows, cols), 1)
    both = jnp.where((t == 2 * k) | (t == 2 * k - 1), 0.5, 0.0)
    return jnp.where((k == 0) & (t == 0), 1.0, both).astype(BF)


def pool_matrix_t(rows, cols):
    t = lax.broadcasted_iota(jnp.int32, (rows, cols), 0)
    k = lax.broadcasted_iota(jnp.int32, (rows, cols), 1)
    both = jnp.where((t == 2 * k) | (t == 2 * k - 1), 0.5, 0.0)
    return jnp.where((k == 0) & (t == 0), 1.0, both).astype(BF)


def proj0_kernel(tok_ref, w_ref, bias_ref, pooled_ref, low_ref, qw_ref, qr_ref, k_ref, v_ref):
    tok = tok_ref[0]
    length = tok.shape[0]
    pooled = mm(pool_matrix(length // 2, length), tok)
    low = pooled.astype(BF)
    pooled_ref[0] = pooled
    low_ref[0] = low
    q = mm(low, w_ref[0, 0])
    qw_ref[0] = (q + bias_ref[0, 0:1, :]).astype(BF)
    qr_ref[0] = (q + bias_ref[0, 1:2, :]).astype(BF)
    k_ref[0] = mm(tok, w_ref[0, 1]).astype(BF)
    v_ref[0] = mm(tok, w_ref[0, 2]).astype(BF)


def proj0(tokens, w_qkv, attn_bias):
    s, length, _ = tokens.shape
    q = length // 2
    seq = lambda i: (i, 0, 0)
    return pl.pallas_call(
        proj0_kernel,
        grid=(s,),
        in_specs=[
            pl.BlockSpec((1, length, D), seq),
            pl.BlockSpec((1, 3, D, D), lambda i: (0, 0, 0, 0)),
            pl.BlockSpec((1, 2, D), lambda i: (0, 0, 0)),
        ],
        out_specs=[pl.BlockSpec((1, q, D), seq)] * 4 + [pl.BlockSpec((1, length, D), seq)] * 2,
        out_shape=[
            sds((s, q, D), F32),
            sds((s, q, D), BF),
            sds((s, q, D), BF),
            sds((s, q, D), BF),
            sds((s, length, D), BF),
            sds((s, length, D), BF),
        ],
        compiler_params=params(),
        cost_estimate=cost(2 * s * length * D * D * 3, 16 * MIB),
        name="proj0",
    )(tokens, w_qkv, attn_bias)


def head_masks():
    lane = lax.broadcasted_iota(jnp.int32, (1, 128), 1)
    first = jnp.where(lane < HEAD_DIM, 1.0, 0.0)
    return first.astype(BF), (1.0 - first).astype(BF)


def both_heads(x, masks):
    return jnp.concatenate([x * masks[0], x * masks[1]], axis=0)


QB = 128


def attn_fwd_kernel(stride, valid_ref, qw_ref, qr_ref, k_ref, v_ref, tab_ref, mixed_ref, p_ref):
    masks = head_masks()
    lane = lax.broadcasted_iota(jnp.int32, (1, 128), 1)
    keys = k_ref.shape[1]
    queries = qw_ref.shape[1]
    width = stride * QB + keys
    valid = valid_ref[0] > 0
    k = k_ref[0]
    v = v_ref[0]
    for b in range(queries // QB):
        rows = slice(b * QB, (b + 1) * QB)
        t0 = stride * (queries - QB - b * QB)
        content = mm_nt(both_heads(qw_ref[0, rows, :], masks), k)
        relative = mm_nt(both_heads(qr_ref[0, rows, :], masks), tab_ref[t0 : t0 + width, :])
        outs = []
        for h in range(2):
            part = slice(h * QB, (h + 1) * QB)
            rolled = pltpu.roll(
                relative[part], width - stride * (QB - 1), 1, stride=stride, stride_axis=0
            )
            scores = (content[part] + rolled[:, :keys]) * SCALE
            scores = jnp.where(valid, scores, MASKED)
            terms = jnp.exp(scores - jnp.max(scores, axis=-1, keepdims=True))
            prob = (terms * (1.0 / jnp.sum(terms, axis=-1, keepdims=True))).astype(BF)
            p_ref[0, h, rows, :] = prob
            outs.append(mm(prob, v))
        mixed_ref[0, rows, :] = jnp.where(lane < HEAD_DIM, outs[0], outs[1]).astype(BF)


def attn_fwd(stride, valid, qw, qr, k, v, tab):
    s, queries, _ = qw.shape
    keys = k.shape[1]
    table = tab.shape[0]
    pair = lambda i, j: (i, 0, j)
    return pl.pallas_call(
        functools.partial(attn_fwd_kernel, stride),
        grid=(s, HEADS // 2),
        in_specs=[
            pl.BlockSpec((1, 1, keys), lambda i, j: (i, 0, 0)),
            pl.BlockSpec((1, queries, 128), pair),
            pl.BlockSpec((1, queries, 128), pair),
            pl.BlockSpec((1, keys, 128), pair),
            pl.BlockSpec((1, keys, 128), pair),
            pl.BlockSpec((table, 128), lambda i, j: (0, j)),
        ],
        out_specs=[
            pl.BlockSpec((1, queries, 128), pair),
            pl.BlockSpec((1, 2, queries, keys), lambda i, j: (i, j, 0, 0)),
        ],
        out_shape=[sds((s, queries, D), BF), sds((s, HEADS, queries, keys), BF)],
        compiler_params=params(),
        cost_estimate=cost(2 * s * HEADS * queries * keys * 64 * 4, 12 * MIB, s * HEADS * queries * keys),
        name="attn_fwd_%d" % stride,
    )(valid, qw, qr, k, v, tab)


def attn_bwd_kernel(
    stride, p_ref, qw_ref, qr_ref, k_ref, v_ref, tab_ref, dm_ref, dq_ref, dk_ref, dv_ref, dtab_ref, dbias_ref
):
    masks = head_masks()
    lane = lax.broadcasted_iota(jnp.int32, (1, 128), 1)
    first = lane < HEAD_DIM
    keys = k_ref.shape[1]
    queries = qw_ref.shape[1]
    width = stride * QB + keys
    flip_i = lax.broadcasted_iota(jnp.int32, (QB, QB), 0)
    flip_j = lax.broadcasted_iota(jnp.int32, (QB, QB), 1)
    flip = jnp.where(flip_i + flip_j == QB - 1, 1.0, 0.0).astype(BF)

    @pl.when(pl.program_id(1) == 0)
    def _():
        dtab_ref[...] = jnp.zeros_like(dtab_ref)
        dbias_ref[...] = jnp.zeros_like(dbias_ref)

    k = k_ref[0]
    v = v_ref[0]
    sum_w = jnp.zeros((1, 128), F32)
    sum_r = jnp.zeros((1, 128), F32)
    dk = jnp.zeros((keys, 128), F32)
    dv = jnp.zeros((keys, 128), F32)
    for b in range(queries // QB):
        rows = slice(b * QB, (b + 1) * QB)
        t0 = stride * (queries - QB - b * QB)
        dm2 = both_heads(dm_ref[0, rows, :], masks)
        qw2 = both_heads(qw_ref[0, rows, :], masks)
        prob = jnp.concatenate([p_ref[0, 0, rows, :], p_ref[0, 1, rows, :]], axis=0)
        dprob = mm_nt(dm2, v)
        wide = prob.astype(F32)
        inner = jnp.sum(dprob * wide, axis=-1, keepdims=True)
        ds = (wide * (dprob - inner)).astype(BF)
        dv = dv + mm_tn(prob, dm2)
        dk = dk + mm_tn(ds, qw2)
        dqw2 = mm(ds, k)
        dqw = jnp.where(first, dqw2[:QB], dqw2[QB:]) * SCALE
        qr_rev = mm(flip, qr_ref[0, rows, :]).astype(BF)
        tab = tab_ref[t0 : t0 + width, :]
        rels = []
        for h in range(2):
            rev = mm(flip, ds[h * QB : (h + 1) * QB])
            padded = jnp.concatenate([rev, jnp.zeros((QB, width - keys), F32)], axis=1)
            rels.append(pltpu.roll(padded, 0, 1, stride=stride, stride_axis=0).astype(BF))
        rel2 = jnp.concatenate(rels, axis=0)
        dtab_ref[t0 : t0 + width, :] += mm_tn(rel2, both_heads(qr_rev, masks)) * SCALE
        dqr2 = mm(rel2, tab)
        dqr_rev = jnp.where(first, dqr2[:QB], dqr2[QB:])
        hi, lo = split_hi_lo(dqr_rev)
        dqr = (mm(flip, hi) + mm(flip, lo)) * SCALE
        dq_ref[0, rows, :] = (dqw + dqr).astype(BF)
        sum_w = sum_w + jnp.sum(dqw, axis=0, keepdims=True)
        sum_r = sum_r + jnp.sum(dqr, axis=0, keepdims=True)
    dk_ref[0] = (dk * SCALE).astype(BF)
    dv_ref[0] = dv.astype(BF)
    dbias_ref[0:1, :] += sum_w
    dbias_ref[1:2, :] += sum_r


def attn_bwd(stride, p, qw, qr, k, v, tab, dmixed):
    s, queries, _ = qw.shape
    keys = k.shape[1]
    table = tab.shape[0]
    pair = lambda j, i: (i, 0, j)
    return pl.pallas_call(
        functools.partial(attn_bwd_kernel, stride),
        grid=(HEADS // 2, s),
        in_specs=[
            pl.BlockSpec((1, 2, queries, keys), lambda j, i: (i, j, 0, 0)),
            pl.BlockSpec((1, queries, 128), pair),
            pl.BlockSpec((1, queries, 128), pair),
            pl.BlockSpec((1, keys, 128), pair),
            pl.BlockSpec((1, keys, 128), pair),
            pl.BlockSpec((table, 128), lambda j, i: (0, j)),
            pl.BlockSpec((1, queries, 128), pair),
        ],
        out_specs=[
            pl.BlockSpec((1, queries, 128), pair),
            pl.BlockSpec((1, keys, 128), pair),
            pl.BlockSpec((1, keys, 128), pair),
            pl.BlockSpec((table, 128), lambda j, i: (0, j)),
            pl.BlockSpec((8, 128), lambda j, i: (0, j)),
        ],
        out_shape=[
            sds((s, queries, D), BF),
            sds((s, keys, D), BF),
            sds((s, keys, D), BF),
            sds((table, D), F32),
            sds((8, D), F32),
        ],
        compiler_params=params(),
        cost_estimate=cost(2 * s * HEADS * queries * keys * 64 * 9, 16 * MIB),
        name="attn_bwd_%d" % stride,
    )(p, qw, qr, k, v, tab, dmixed)


def ffn_fwd_kernel(
    mixed_ref, resid_ref, wout_ref, wup_ref, wdown_ref, wqkv_ref, abias_ref, upb_ref, gain_ref, nbias_ref, obias_ref,
    hid_ref, x1_ref, r1_ref, act_ref, slope_ref, x2_ref, r2_ref, out_ref, low_ref, qw_ref, qr_ref, k_ref, v_ref,
):
    pre_norm = resid_ref[...] + (mm(mixed_ref[...], wout_ref[0]) + obias_ref[0, 0:1, :])
    x1, r1 = ln_fwd(pre_norm)
    x1_ref[...] = x1
    r1_ref[...] = jnp.broadcast_to(r1, r1_ref.shape)
    hidden = x1 * gain_ref[0, 0:1, :] + nbias_ref[0, 0:1, :]
    low = hidden.astype(BF)
    hid_ref[...] = low
    total = jnp.zeros_like(hidden)
    for c in range(PANELS):
        cols = slice(c * D, (c + 1) * D)
        act, slope = gelu_and_slope(mm(low, wup_ref[0, :, cols]) + upb_ref[0:1, cols])
        act = act.astype(BF)
        act_ref[:, cols] = act
        slope_ref[:, cols] = slope.astype(BF)
        total = total + mm(act, wdown_ref[0, cols, :])
    x2, r2 = ln_fwd(hidden + (total + obias_ref[0, 1:2, :]))
    x2_ref[...] = x2
    r2_ref[...] = jnp.broadcast_to(r2, r2_ref.shape)
    out = x2 * gain_ref[0, 1:2, :] + nbias_ref[0, 1:2, :]
    out_ref[...] = out
    olow = out.astype(BF)
    low_ref[...] = olow
    q = mm(olow, wqkv_ref[0, 0])
    qw_ref[...] = (q + abias_ref[0, 0:1, :]).astype(BF)
    qr_ref[...] = (q + abias_ref[0, 1:2, :]).astype(BF)
    k_ref[...] = mm(olow, wqkv_ref[0, 1]).astype(BF)
    v_ref[...] = mm(olow, wqkv_ref[0, 2]).astype(BF)


def ffn_fwd(mixed, resid, w_out, w_up, w_down, w_qkv, attn_bias, up_bias, gain, nbias, obias):
    rows = mixed.shape[0]
    blk = min(256, rows)
    row = lambda i: (i, 0)
    one = lambda l: (lambda i: (l, 0, 0))
    single = dict(pipeline_mode=pl.Buffered(1))
    wide = lambda n: pl.BlockSpec((blk, n), row)
    return pl.pallas_call(
        ffn_fwd_kernel,
        grid=(rows // blk,),
        in_specs=[
            wide(D),
            wide(D),
            pl.BlockSpec((1, D, D), one(0), **single),
            pl.BlockSpec((1, D, FF), one(0), **single),
            pl.BlockSpec((1, FF, D), one(0), **single),
            pl.BlockSpec((1, 3, D, D), lambda i: (1, 0, 0, 0), **single),
            pl.BlockSpec((1, 2, D), one(1)),
            pl.BlockSpec((2, FF), lambda i: (0, 0)),
            pl.BlockSpec((1, 2, D), one(0)),
            pl.BlockSpec((1, 2, D), one(0)),
            pl.BlockSpec((1, 2, D), one(0)),
        ],
        out_specs=[wide(D), wide(D), wide(128), wide(FF), wide(FF), wide(D), wide(128)] + [wide(D)] * 6,
        out_shape=[
            sds((rows, D), BF),
            sds((rows, D), F32),
            sds((rows, 128), F32),
            sds((rows, FF), BF),
            sds((rows, FF), BF),
            sds((rows, D), F32),
            sds((rows, 128), F32),
            sds((rows, D), F32),
            sds((rows, D), BF),
            sds((rows, D), BF),
            sds((rows, D), BF),
            sds((rows, D), BF),
            sds((rows, D), BF),
        ],
        compiler_params=params(),
        cost_estimate=cost(2 * rows * D * D * 12, 34 * MIB, rows * FF),
        name="ffn_fwd",
    )(mixed, resid, w_out, w_up, w_down, w_qkv, attn_bias, up_bias, gain, nbias, obias)


def bases(info_ref, rows_each):
    me, side = info_ref[0], info_ref[1]
    order_x, order_s = {}, {}
    for r in range(SHARDS):
        rel = jnp.bitwise_xor(me, r)
        b0 = jnp.bitwise_and(rel, 1)
        b1 = jnp.bitwise_and(jnp.right_shift(rel, 1), 1)
        b2 = jnp.bitwise_and(jnp.right_shift(rel, 2), 1)
        b3 = jnp.bitwise_and(jnp.right_shift(rel, 3), 1)
        for half in range(2):
            s = jnp.bitwise_xor(side, half)
            tail = b2 * 2 + b3
            order_x[r, half] = (((b0 * 2 + b1) * 2 + s) * 4 + tail) * rows_each
            order_s[r, half] = (((b0 * 2 + s) * 2 + b1) * 4 + tail) * rows_each
    return order_x, order_s


def put(buf_ref, base, offset, tile, shards, rows):
    low = tile.astype(BF)
    for n, r in enumerate(shards):
        for half in range(2):
            start = pl.multiple_of(base[r, half] + offset, 16)
            buf_ref[pl.ds(start, rows), :] = low[n * rows : (n + 1) * rows, half * HALF : (half + 1) * HALF]


def ship(buf_ref, keep_ref, send_ref, sems):
    n = keep_ref.shape[0]
    copies = [
        pltpu.make_async_copy(buf_ref.at[pl.ds(n, n)], send_ref, sems.at[0]),
        pltpu.make_async_copy(buf_ref.at[pl.ds(0, n)], keep_ref, sems.at[1]),
    ]
    for copy in copies:
        copy.start()
    return copies


def ffn_back(
    info_ref, dy, x2, r2, gain2, gain1, wout_ref, wup, wdown, act, slope, hid_ref, x1, r1, mixed_ref,
    small_ref, upg_ref, dmixed_ref, dbranch_ref, dres_ref, dpost_ref, dhid_ref, buf_a, buf_b, outs, sems,
):
    small_ref[...] = jnp.zeros_like(small_ref)
    dpost = ln_bwd(dy, x2, r2, gain2)
    small_ref[1:2, :] = jnp.sum(dy * x2, axis=0, keepdims=True)
    small_ref[3:4, :] = jnp.sum(dy, axis=0, keepdims=True)
    dffn = dpost.astype(BF)
    small_ref[5:6, :] = jnp.sum(dffn.astype(F32), axis=0, keepdims=True)
    dpost_ref[...] = dffn
    dhid_ref[...] = dpost
    order_x, order_s = bases(info_ref, UP_ROWS)
    for c in range(PANELS):
        cols = slice(c * D, (c + 1) * D)
        dffn = dpost_ref[...]
        dact = mm_nt(dffn, wdown[cols, :])
        put(buf_b, order_s, 0, mm_tn(act[:, cols], dffn), range(4 * c, 4 * c + 4), UP_ROWS)
        dpre = (dact * slope[:, cols].astype(F32)).astype(BF)
        upg_ref[:, cols] = jnp.broadcast_to(jnp.sum(dpre.astype(F32), axis=0, keepdims=True), (8, D))
        dhid_ref[...] += mm_nt(dpre, wup[:, cols])
        put(buf_a, order_x, c * ROW, mm_tn(hid_ref[...], dpre), range(SHARDS), ROW)
    copies = ship(buf_a, outs[0], outs[1], [sems.at[0], sems.at[1]]) if False else None
    n = outs[0].shape[0]
    copies = [
        pltpu.make_async_copy(buf_a.at[pl.ds(n, n)], outs[1], sems.at[0]),
        pltpu.make_async_copy(buf_b.at[pl.ds(n, n)], outs[3], sems.at[1]),
        pltpu.make_async_copy(buf_a.at[pl.ds(0, n)], outs[0], sems.at[2]),
        pltpu.make_async_copy(buf_b.at[pl.ds(0, n)], outs[2], sems.at[3]),
    ]
    for copy in copies:
        copy.start()
    dhid = dhid_ref[...]
    xh = x1()
    small_ref[0:1, :] = jnp.sum(dhid * xh, axis=0, keepdims=True)
    small_ref[2:3, :] = jnp.sum(dhid, axis=0, keepdims=True)
    dres = ln_bwd(dhid, xh, r1(), gain1)
    dres_ref[...] = dres
    dbranch = dres.astype(BF)
    dbranch_ref[...] = dbranch
    small_ref[4:5, :] = jnp.sum(dbranch.astype(F32), axis=0, keepdims=True)
    dmixed_ref[...] = mm_nt(dbranch, wout_ref[0]).astype(BF)
    for copy in copies:
        copy.wait()


def ffn_last_kernel(
    info_ref, mixed_ref, resid_ref, cot_ref, wout_ref, wup_hbm, wdown_hbm, upb_ref, gain_ref, nbias_ref, obias_ref,
    lout_ref, dmixed_ref, dbranch_ref, dres_ref, small_ref, upg_ref, ka, sa, kb, sb,
    wup, wdown, act, slope, hid, x1s, dffn_s, dhid_s, buf_a, buf_b, sems,
):
    cp_up = pltpu.make_async_copy(wup_hbm.at[1], wup, sems.at[4])
    cp_down = pltpu.make_async_copy(wdown_hbm.at[1], wdown, sems.at[5])
    cp_up.start()
    cp_down.start()
    pre_norm = resid_ref[...] + (mm(mixed_ref[...], wout_ref[0]) + obias_ref[0, 0:1, :])
    x1, r1 = ln_fwd(pre_norm)
    x1s[...] = x1
    hidden = x1 * gain_ref[0, 0:1, :] + nbias_ref[0, 0:1, :]
    hid[...] = hidden.astype(BF)
    dhid_s[...] = hidden + obias_ref[0, 1:2, :]
    cp_up.wait()
    cp_down.wait()
    for c in range(PANELS):
        cols = slice(c * D, (c + 1) * D)
        a, s = gelu_and_slope(mm(hid[...], wup[:, cols]) + upb_ref[1:2, cols])
        a = a.astype(BF)
        act[:, cols] = a
        slope[:, cols] = s.astype(BF)
        dhid_s[...] += mm(a, wdown[cols, :])
    x2, r2 = ln_fwd(dhid_s[...])
    lout_ref[...] = (x2 * gain_ref[0, 1:2, :] + nbias_ref[0, 1:2, :]).astype(BF)
    dy = cot_ref[...].astype(F32)
    ffn_back(
        info_ref, dy, x2, r2, gain_ref[0, 1:2, :], gain_ref[0, 0:1, :], wout_ref, wup, wdown, act, slope, hid,
        lambda: x1s[...], lambda: r1, mixed_ref, small_ref, upg_ref, dmixed_ref, dbranch_ref, dres_ref, dffn_s, dhid_s,
        buf_a, buf_b, (ka, sa, kb, sb), sems,
    )


BUF_ROWS = 2 * SHARDS * UP_ROWS


def ffn_last(info, mixed, resid, cot, w_out, w_up, w_down, up_bias, gain, nbias, obias):
    rows = mixed.shape[0]
    layer = lambda: pl.BlockSpec((1, 2, D), lambda i, n: (1, 0, 0))
    whole = pl.BlockSpec((rows, D), lambda i, n: (0, 0))
    return pl.pallas_call(
        ffn_last_kernel,
        grid_spec=pltpu.PrefetchScalarGridSpec(
            num_scalar_prefetch=1,
            grid=(1,),
            in_specs=[
                whole, whole, whole,
                pl.BlockSpec((1, D, D), lambda i, n: (1, 0, 0)),
                ANY, ANY,
                pl.BlockSpec((2, FF), lambda i, n: (0, 0)),
                layer(), layer(), layer(),
            ],
            out_specs=[whole, whole, whole, whole,
                       pl.BlockSpec((8, D), lambda i, n: (0, 0)), pl.BlockSpec((8, FF), lambda i, n: (0, 0)),
                       ANY, ANY, ANY, ANY],
            scratch_shapes=[
                pltpu.VMEM((D, FF), BF), pltpu.VMEM((FF, D), BF),
                pltpu.VMEM((rows, FF), BF), pltpu.VMEM((rows, FF), BF),
                pltpu.VMEM((rows, D), BF), pltpu.VMEM((rows, D), F32),
                pltpu.VMEM((rows, D), BF), pltpu.VMEM((rows, D), F32),
                pltpu.VMEM((BUF_ROWS, HALF), BF), pltpu.VMEM((BUF_ROWS, HALF), BF),
                pltpu.SemaphoreType.DMA((6,)),
            ],
        ),
        out_shape=[
            sds((rows, D), BF), sds((rows, D), BF), sds((rows, D), BF), sds((rows, D), F32),
            sds((8, D), F32), sds((8, FF), F32),
        ] + [sds((BUF_ROWS // 2, HALF), BF)] * 4,
        compiler_params=params(),
        cost_estimate=cost(2 * rows * D * D * 26, 30 * MIB, rows * FF),
        name="ffn_last",
    )(info, mixed, resid, cot, w_out, w_up, w_down, up_bias, gain, nbias, obias)


def ffn_bwd_kernel(
    info_ref, dy_ref, x2_ref, r2_ref, mixed_ref, hid_ref, x1_ref, r1_ref, gain_ref, wout_ref,
    wup_hbm, wdown_hbm, act_hbm, slope_hbm,
    dmixed_ref, dbranch_ref, dres_ref, small_ref, upg_ref, ka, sa, kb, sb,
    wup, wdown, act, slope, dffn_s, dhid_s, buf_a, buf_b, sems,
):
    loads = [
        pltpu.make_async_copy(wdown_hbm.at[0], wdown, sems.at[4]),
        pltpu.make_async_copy(act_hbm, act, sems.at[5]),
        pltpu.make_async_copy(slope_hbm, slope, sems.at[6]),
        pltpu.make_async_copy(wup_hbm.at[0], wup, sems.at[7]),
    ]
    for copy in loads:
        copy.start()
    dy = dy_ref[...]
    for copy in loads:
        copy.wait()
    ffn_back(
        info_ref, dy, x2_ref[...], r2_ref[:, 0:1], gain_ref[0, 1:2, :], gain_ref[0, 0:1, :], wout_ref, wup, wdown,
        act, slope, hid_ref, lambda: x1_ref[...], lambda: r1_ref[:, 0:1], mixed_ref, small_ref, upg_ref,
        dmixed_ref, dbranch_ref, dres_ref, dffn_s, dhid_s, buf_a, buf_b, (ka, sa, kb, sb), sems,
    )


def ffn_bwd(info, dy, x2, r2, mixed, hid, x1, r1, gain, w_out, w_up, w_down, act, slope):
    rows = mixed.shape[0]
    whole = pl.BlockSpec((rows, D), lambda i, n: (0, 0))
    thin = pl.BlockSpec((rows, 128), lambda i, n: (0, 0))
    return pl.pallas_call(
        ffn_bwd_kernel,
        grid_spec=pltpu.PrefetchScalarGridSpec(
            num_scalar_prefetch=1,
            grid=(1,),
            in_specs=[
                whole, whole, thin, whole, whole, whole, thin,
                pl.BlockSpec((1, 2, D), lambda i, n: (0, 0, 0)),
                pl.BlockSpec((1, D, D), lambda i, n: (0, 0, 0)),
                ANY, ANY, ANY, ANY,
            ],
            out_specs=[whole, whole, whole,
                       pl.BlockSpec((8, D), lambda i, n: (0, 0)), pl.BlockSpec((8, FF), lambda i, n: (0, 0)),
                       ANY, ANY, ANY, ANY],
            scratch_shapes=[
                pltpu.VMEM((D, FF), BF), pltpu.VMEM((FF, D), BF),
                pltpu.VMEM((rows, FF), BF), pltpu.VMEM((rows, FF), BF),
                pltpu.VMEM((rows, D), BF), pltpu.VMEM((rows, D), F32),
                pltpu.VMEM((BUF_ROWS, HALF), BF), pltpu.VMEM((BUF_ROWS, HALF), BF),
                pltpu.SemaphoreType.DMA((8,)),
            ],
        ),
        out_shape=[
            sds((rows, D), BF), sds((rows, D), BF), sds((rows, D), F32),
            sds((8, D), F32), sds((8, FF), F32),
        ] + [sds((BUF_ROWS // 2, HALF), BF)] * 4,
        compiler_params=params(),
        cost_estimate=cost(2 * rows * D * D * 17, 36 * MIB),
        name="ffn_bwd",
    )(info, dy, x2, r2, mixed, hid, x1, r1, gain, w_out, w_up, w_down, act, slope)


def first_back_kernel(dres_ref, dq_ref, dk_ref, dv_ref, w_ref, out_ref):
    out_ref[...] = dres_ref[...] + (
        mm_nt(dq_ref[...], w_ref[0, 0]) + mm_nt(dk_ref[...], w_ref[0, 1]) + mm_nt(dv_ref[...], w_ref[0, 2])
    )


def first_back(dres, dq, dk, dv, w_qkv):
    rows = dres.shape[0]
    row = lambda i: (i, 0)
    blk = 256
    wide = pl.BlockSpec((blk, D), row)
    return pl.pallas_call(
        first_back_kernel,
        grid=(rows // blk,),
        in_specs=[wide] * 4 + [pl.BlockSpec((1, 3, D, D), lambda i: (1, 0, 0, 0), pipeline_mode=pl.Buffered(1))],
        out_specs=wide,
        out_shape=sds((rows, D), F32),
        compiler_params=params(),
        cost_estimate=cost(2 * rows * D * D * 3, 8 * MIB),
        name="first_back",
    )(dres, dq, dk, dv, w_qkv)


def tokens_back_kernel(dres_ref, dq_ref, dk_ref, dv_ref, w_ref, out_ref):
    dpool = dres_ref[0] + mm_nt(dq_ref[0], w_ref[0, 0])
    hi, lo = split_hi_lo(dpool)
    spread = pool_matrix_t(dk_ref.shape[1], dpool.shape[0])
    out_ref[0] = mm_nt(dk_ref[0], w_ref[0, 1]) + mm_nt(dv_ref[0], w_ref[0, 2]) + (mm(spread, hi) + mm(spread, lo))


def tokens_back(dres, dq, dk, dv, w_qkv):
    s, length, _ = dk.shape
    queries = dq.shape[1]
    seq = lambda i: (i, 0, 0)
    return pl.pallas_call(
        tokens_back_kernel,
        grid=(s,),
        in_specs=[
            pl.BlockSpec((1, queries, D), seq),
            pl.BlockSpec((1, queries, D), seq),
            pl.BlockSpec((1, length, D), seq),
            pl.BlockSpec((1, length, D), seq),
            pl.BlockSpec((1, 3, D, D), lambda i: (0, 0, 0, 0)),
        ],
        out_specs=pl.BlockSpec((1, length, D), seq),
        out_shape=sds((s, length, D), F32),
        compiler_params=params(),
        cost_estimate=cost(2 * s * length * D * D * 3, 14 * MIB),
        name="tokens_back",
    )(dres, dq, dk, dv, w_qkv)


A_MATS = 3
B_MATS = 2


def qkv_grad_kernel(
    info_ref, xq_ref, xk_ref, dq_ref, dk_ref, dv_ref, mixed_ref, dbranch_ref, enc_ref, dtab_ref,
    ka, sa, kb, sb, buf_a, buf_b, sems,
):
    order_x, _ = bases(info_ref, A_MATS * ROW)
    _, order_s = bases(info_ref, B_MATS * ROW)
    every = range(SHARDS)
    put(buf_a, order_x, 0, mm_tn(mixed_ref[...], dbranch_ref[...]), every, ROW)
    put(buf_a, order_x, ROW, mm_tn(xq_ref[...], dq_ref[...]), every, ROW)
    put(buf_a, order_x, 2 * ROW, mm_tn(xk_ref[...], dk_ref[...]), every, ROW)
    put(buf_b, order_s, 0, mm_tn(xk_ref[...], dv_ref[...]), every, ROW)
    put(buf_b, order_s, ROW, mm_tn(enc_ref[...], dtab_ref[...].astype(BF)), every, ROW)
    n, m = ka.shape[0], kb.shape[0]
    copies = [
        pltpu.make_async_copy(buf_a.at[pl.ds(n, n)], sa, sems.at[0]),
        pltpu.make_async_copy(buf_b.at[pl.ds(m, m)], sb, sems.at[1]),
        pltpu.make_async_copy(buf_a.at[pl.ds(0, n)], ka, sems.at[2]),
        pltpu.make_async_copy(buf_b.at[pl.ds(0, m)], kb, sems.at[3]),
    ]
    for copy in copies:
        copy.start()
    for copy in copies:
        copy.wait()


def qkv_grad(info, xq, xk, dq, dk, dv, mixed, dbranch, enc, dtab):
    whole = lambda x: pl.BlockSpec(x.shape, lambda i, n: (0, 0))
    ins = (xq, xk, dq, dk, dv, mixed, dbranch, enc, dtab)
    n, m = SHARDS * A_MATS * ROW, SHARDS * B_MATS * ROW
    return pl.pallas_call(
        qkv_grad_kernel,
        grid_spec=pltpu.PrefetchScalarGridSpec(
            num_scalar_prefetch=1,
            grid=(1,),
            in_specs=[whole(x) for x in ins],
            out_specs=[ANY, ANY, ANY, ANY],
            scratch_shapes=[
                pltpu.VMEM((2 * n, HALF), BF), pltpu.VMEM((2 * m, HALF), BF), pltpu.SemaphoreType.DMA((4,)),
            ],
        ),
        out_shape=[sds((n, HALF), BF)] * 2 + [sds((m, HALF), BF)] * 2,
        compiler_params=params(),
        cost_estimate=cost(2 * D * D * (2 * xq.shape[0] + 2 * xk.shape[0] + enc.shape[0]), 16 * MIB),
        name="qkv_grad",
    )(info, *ins)


def swap(x, axis, bit):
    n = lax.axis_size(axis)
    return lax.ppermute(x, axis, [(i, i ^ bit) for i in range(n)])


def halving(keep, send, steps):
    total = keep + swap(send, *steps[0])
    for step in steps[1:]:
        n = total.shape[0] // 2
        total = total[:n] + swap(total[n:], *step)
    return total


X_FIRST = (("rows", 1), ("rows", 2), ("seq", 1), ("rows", 4), ("rows", 8))
S_FIRST = (("rows", 1), ("seq", 1), ("rows", 2), ("rows", 4), ("rows", 8))


def reduce_stream(keep, send, order, side):
    mine = halving(keep, send, order)
    other = swap(mine, "seq", 1)
    low = jnp.where(side == 0, mine, other)
    high = jnp.where(side == 0, other, mine)
    return jnp.concatenate([low, high], axis=1).astype(F32)


def generic_stream(keep, send, order, mats):
    both = jnp.concatenate([keep, send], axis=0)
    if order is X_FIRST:
        view = both.reshape(2, 2, 2, 2, 2, mats, -1, HALF)
        view = view.transpose(5, 4, 3, 1, 0, 6, 2, 7)
    else:
        view = both.reshape(2, 2, 2, 2, 2, mats, -1, HALF)
        view = view.transpose(5, 4, 3, 2, 0, 6, 1, 7)
    whole = view.reshape(mats, -1, D)
    mine = lax.psum_scatter(whole, "rows", scatter_dimension=1, tiled=True)
    return lax.psum(mine.astype(F32), "seq").reshape(-1, D)


def all_sum(x):
    for step in X_FIRST:
        x = x + swap(x, *step)
    return x


def sinusoid(distance):
    half_width = D // 2
    frequency = 10000.0 ** (-jnp.arange(half_width, dtype=F32) / half_width)
    angles = distance.astype(F32)[:, None] * frequency[None, :]
    return jnp.concatenate([jnp.sin(angles), jnp.cos(angles)], axis=1)


def to_sequences(x, side, parts):
    own = x.shape[0] // parts
    mine = lax.dynamic_slice_in_dim(x, side * own, own, 0)
    other = swap(lax.dynamic_slice_in_dim(x, (1 - side) * own, own, 0), "seq", 1)
    return jnp.where(
        side == 0, jnp.concatenate([mine, other], axis=1), jnp.concatenate([other, mine], axis=1)
    )


def to_positions(x, side, parts, wire=None):
    own = x.shape[1] // parts
    mine = lax.dynamic_slice_in_dim(x, side * own, own, 1)
    sent = lax.dynamic_slice_in_dim(x, (1 - side) * own, own, 1)
    other = swap(sent if wire is None else sent.astype(wire), "seq", 1).astype(x.dtype)
    return jnp.where(
        side == 0, jnp.concatenate([mine, other], axis=0), jnp.concatenate([other, mine], axis=0)
    )


def on_device(
    tokens, lengths, key_mask, cotangent, w_qkv, w_out, w_pos, w_up, w_down, attn_bias, up_bias, norm_gain,
    norm_bias, out_bias,
):
    side = lax.axis_index("seq")
    parts = lax.axis_size("seq")
    n_rows = lax.axis_size("rows")
    me = lax.axis_index("rows")
    halved = n_rows == SHARDS and parts == 2
    zero = jnp.int32(0)
    info = jnp.stack([me, side]) if halved else jnp.stack([zero, zero])
    info = info.astype(jnp.int32)

    tok = to_sequences(tokens, side, parts)
    cot = to_sequences(cotangent, side, parts)
    seqs, length, _ = tok.shape
    queries = length // 2
    mine = lambda x: lax.dynamic_slice_in_dim(x, side * seqs, seqs, 0)
    places = jnp.arange(length, dtype=jnp.int32)[None, :]
    key_valid = jnp.where(places < mine(lengths)[:, None], mine(key_mask), 0)
    shifted_valid = jnp.concatenate([key_valid[:, :1], key_valid[:, :-1]], axis=1)
    pooled_valid = jnp.max(shifted_valid.reshape(seqs, queries, 2), axis=2)

    enc0 = sinusoid(2 * (queries - 1) - jnp.arange(2 * length, dtype=jnp.int32)).astype(BF)
    enc1 = enc0[::2]
    tab0 = mm(enc0, w_pos[0]).astype(BF)
    tab1 = mm(enc1, w_pos[1]).astype(BF)

    flat = lambda x: x.reshape(-1, x.shape[-1])
    sets = lambda x: x.reshape(seqs, -1, D)

    pooled, pooled_low, qw0, qr0, k0, v0 = proj0(tok, w_qkv, attn_bias)
    mixed0, p0 = attn_fwd(2, key_valid[:, None, :], qw0, qr0, k0, v0, tab0)
    mixed0 = flat(mixed0)
    hid, x1, r1, act, slope, x2, r2, first, first_low, qw1, qr1, k1, v1 = ffn_fwd(
        mixed0, flat(pooled), w_out, w_up, w_down, w_qkv, attn_bias, up_bias, norm_gain, norm_bias, out_bias
    )
    qw1, qr1, k1, v1 = sets(qw1), sets(qr1), sets(k1), sets(v1)
    mixed1, p1 = attn_fwd(1, pooled_valid[:, None, :], qw1, qr1, k1, v1, tab1)
    mixed1 = flat(mixed1)
    lout, dmixed1, dbranch1, dres1, small1, upg1, ka1, sa1, kb1, sb1 = ffn_last(
        info, mixed1, first, flat(cot), w_out, w_up, w_down, up_bias, norm_gain, norm_bias, out_bias
    )
    dq1, dk1, dv1, dtab1, dbias1 = attn_bwd(1, p1, qw1, qr1, k1, v1, tab1, sets(dmixed1))
    dq1, dk1, dv1 = flat(dq1), flat(dk1), flat(dv1)
    dfirst = first_back(dres1, dq1, dk1, dv1, w_qkv)
    ja1, ta1, jb1, tb1 = qkv_grad(info, first_low, first_low, dq1, dk1, dv1, mixed1, dbranch1, enc1, dtab1)
    dmixed0, dbranch0, dres0, small0, upg0, ka0, sa0, kb0, sb0 = ffn_bwd(
        info, dfirst, x2, r2, mixed0, hid, x1, r1, norm_gain, w_out, w_up, w_down, act, slope
    )
    dq0, dk0, dv0, dtab0, dbias0 = attn_bwd(2, p0, qw0, qr0, k0, v0, tab0, sets(dmixed0))
    dtok = tokens_back(sets(dres0), dq0, dk0, dv0, w_qkv)
    ja0, ta0, jb0, tb0 = qkv_grad(
        info, flat(pooled_low), flat(tok), flat(dq0), flat(dk0), flat(dv0), mixed0, dbranch0, enc0, dtab0
    )

    if halved:
        stream = lambda k, s, order, mats: reduce_stream(k, s, order, side)
    else:
        stream = generic_stream
    up1 = stream(ka1, sa1, X_FIRST, PANELS)
    down1 = stream(kb1, sb1, S_FIRST, 1)
    att_a1 = stream(ja1, ta1, X_FIRST, A_MATS)
    att_b1 = stream(jb1, tb1, S_FIRST, B_MATS)
    up0 = stream(ka0, sa0, X_FIRST, PANELS)
    down0 = stream(kb0, sb0, S_FIRST, 1)
    att_a0 = stream(ja0, ta0, X_FIRST, A_MATS)
    att_b0 = stream(jb0, tb0, S_FIRST, B_MATS)

    small = lambda s, u, b: jnp.concatenate([s[:6], b[:2], u[0].reshape(PANELS, D)], axis=0)
    if halved:
        sums = jnp.stack([all_sum(small(small0, upg0, dbias0)), all_sum(small(small1, upg1, dbias1))])
    else:
        sums = lax.psum(jnp.stack([small(small0, upg0, dbias0), small(small1, upg1, dbias1)]), ("rows", "seq"))
    own = D // n_rows
    cut = lambda x: lax.dynamic_slice_in_dim(x, me * own, own, 2)
    upb = lax.dynamic_slice_in_dim(sums[:, 8:].reshape(2, FF), me * (FF // n_rows), FF // n_rows, 1)

    thirds = lambda x: x.reshape(A_MATS, -1, D)
    pairs = lambda x: x.reshape(B_MATS, -1, D)
    a0, a1, b0, b1 = thirds(att_a0), thirds(att_a1), pairs(att_b0), pairs(att_b1)
    panels = lambda x: jnp.concatenate(list(x.reshape(PANELS, -1, D)), axis=1)
    return (
        to_positions(sets(lout), side, parts),
        to_positions(dtok, side, parts, BF),
        jnp.stack([jnp.stack([a0[1], a0[2], b0[0]]), jnp.stack([a1[1], a1[2], b1[0]])]),
        jnp.stack([a0[0], a1[0]]),
        jnp.stack([b0[1], b1[1]]),
        jnp.stack([panels(up0), panels(up1)]),
        jnp.stack([down0, down1]),
        cut(sums[:, 6:8]),
        upb,
        cut(sums[:, 0:2]),
        cut(sums[:, 2:4]),
        cut(sums[:, 4:6]),
    )


def solution(mesh):
    seq3 = P("rows", "seq", None)
    in_specs = (seq3, P("rows"), P("rows", None), seq3) + (P(),) * 10
    mat = P(None, "rows", None)
    vec = P(None, None, "rows")
    out_specs = (seq3, seq3, P(None, None, "rows", None), mat, mat, mat, mat, vec, P(None, "rows"), vec, vec, vec)
    return jax.shard_map(on_device, mesh=mesh, in_specs=in_specs, out_specs=out_specs, check_vma=False)
```

time: 1460 us -> 517 us (0.35)
  waiting for transfers between devices: 695 us -> 171 us
  local copies, waits for them, and re-layouts: 310 us -> 23 us
  matrix products: 233 us -> 7.01 us
  Pallas kernels: 0 us -> 213 us
  blocking collectives: 95.5 us -> 0 us
  other arithmetic: 90.1 us -> 28.2 us
  starting transfers between devices: 7.67 us -> 63.3 us
    reduce_scatter x9 -> x0, waiting for transfers between devices: 694 us -> none  [the longest x1 200 us: on_device(): lax.psum_scatter(grad_up, ('rows', 'seq'), scatter_dimension=1, tiled=True)]
    dot_general x58 -> x2, matrix products: 233 us -> 7.01 us  [mm(): lax.dot_general(a, b, (((1,), (0,)), ((), ())), preferred_element_type=F32)]
    pallas_call x0 -> x12, Pallas kernels: none -> 213 us  [the longest x2 51.6 us: attn_bwd(): pl.pallas_call(functools.partial(attn_bwd_kernel, stride), grid=(HEADS //...]
    ppermute x2 -> x62, waiting for transfers between devices: 0.01 us -> 171 us  [swap(): return lax.ppermute(x, axis, [(i, i ^ bit) for i in range(n)])]
    reshape x21 -> x1, local copies, waits for them, and re-layouts: 159 us -> 0.2 us  [on_device(): pooled_valid = jnp.max(shifted_valid.reshape(seqs, queries, 2), axis=2)]
    ppermute x2 -> x62, starting transfers between devices: 6.3 us -> 63.3 us  [swap(): return lax.ppermute(x, axis, [(i, i ^ bit) for i in range(n)])]
    all_gather x10 -> x0, blocking collectives: 55.4 us -> none  [the longest x1 8.24 us: on_device(): lax.all_gather(sum_down.astype(jnp.bfloat16), 'seq', axis=1, tiled=True)]
    unnamed x1 -> x0, blocking collectives: 40.1 us -> none
  transfers between devices with their start and end apart: 16 -> 62, of which waited for: 5 -> 37; matrix products, arithmetic and copies ran while one was open for 35% -> 9% of each run, Pallas kernels for 0% -> 19%
where the time goes in v1:
time: 517 us; the launch traced here: 507 us
  Pallas kernels  213 us (41%)
  waiting for transfers between devices  171 us (33%)
  starting transfers between devices  63.3 us (12%)
  other arithmetic  28.2 us (5%)
  local copies, waits for them, and re-layouts  23 us (4%)
  matrix products  7.01 us (1%)
    ppermute x62, waiting for transfers between devices, swap(): return lax.ppermute(x, axis, [(i, i ^ bit) for i in range(n)])  171 us
    ppermute x62, starting transfers between devices, swap(): return lax.ppermute(x, axis, [(i, i ^ bit) for i in range(n)])  63.3 us
    pallas_call x2, Pallas kernels, attn_bwd(): pl.pallas_call(functools.partial(attn_bwd_kernel, stride), grid=(HEADS //...  51.6 us
    pallas_call x2, Pallas kernels, attn_fwd(): pl.pallas_call(functools.partial(attn_fwd_kernel, stride), grid=(s, HEADS...  38.3 us
    pallas_call x1, Pallas kernels, ffn_last(): pl.pallas_call(ffn_last_kernel, grid_spec=pltpu.PrefetchScalarGridSpec(nu...  30.9 us
    pallas_call x1, Pallas kernels, ffn_bwd(): pl.pallas_call(ffn_bwd_kernel, grid_spec=pltpu.PrefetchScalarGridSpec(num...  27 us
    pallas_call x2, Pallas kernels, qkv_grad(): pl.pallas_call(qkv_grad_kernel, grid_spec=pltpu.PrefetchScalarGridSpec(nu...  22.6 us
    pallas_call x1, Pallas kernels, ffn_fwd(): pl.pallas_call(ffn_fwd_kernel, grid=(rows // blk,), in_specs=[wide(D), wi...  19.7 us
  transfers between devices with their start and end apart: 62, of which 37 were waited for; matrix products, arithmetic and copies ran while one was open for 9% of the time, Pallas kernels for 19%

profile of v1, /device:TPU:0, one launch (start us, length us, event | category | flops | bytes accessed | tf_op | source)
XLA Modules:
  0.0 507.4 jit_solution(13129177117703021208)
XLA Ops:
  7.0 6.3 %fusion = (bf16[1024,384]{1,0:T(8,128)(2,1)S(1)}, bf16[1024,384]{1,0:T(8,128)(2,1)S(1)}) fusion(f32[384]{0:T(512)S(1)} %multiply_power_fusion, f32[1024]{0:T(1024)S(1)} %subtract_convert_fusion), kind=kLoop, calls=%fused_computation.4 | loop fusion | flops 1179648 | bytes 1578496 | tf_op jit(solution)/shard_map/convert.1
  35.0 7.9 %proj0.1 = (f32[2,256,768]{2,1,0:T(8,128)}, bf16[2,256,768]{2,1,0:T(8,128)(2,1)}, bf16[2,256,768]{2,1,0:T(8,128)(2,1)}, bf16[2,256,768]{2,1,0:T(8,128)(2,1)}, bf...) custom-call(bf16[2,512,768]{2,1,0:T(8,128)(2,1)} %maximum_select_fusion.1.tok_ref, ...), custom_call_target="tpu_custom_call" | custom-call | flops 3623878656 | bytes 16777216 | tf_op jit(solution)/shard_map/proj0/pallas_call | solution.py:124
  42.9 21.4 %attn_fwd_2.1 = (bf16[2,256,768]{2,1,0:T(8,128)(2,1)}, bf16[2,12,256,512]{3,2,1,0:T(8,128)(2,1)}) custom-call(s32[2,1,512]{2,1,0:T(1,128)} %broadcast_in_dim.16.valid_ref, bf16[2,256,768]{2,1,0:T(8,128)(2,1)} %get-tuple-element.72.qw_ref, bf16[2,256,768]{2,1,0:T(8,128)(2,1)} %get-tuple-element.73.qr_ref, bf16[2,512,768]{2,1,0:T(8,128)(2,1)} %get-tuple-element.74.k_ref, ...), custom_call_target="tpu_custom_call" | custom-call | flops 1610612736 | bytes 12582912 | tf_op jit(solution)/shard_map/attn_fwd_2/pallas_call | solution.py:194
  64.3 19.7 %ffn_fwd.1 = (bf16[512,768]{1,0:T(8,128)(2,1)}, f32[512,768]{1,0:T(8,128)}, f32[512,128]{1,0:T(8,128)}, bf16[512,3072]{1,0:T(8,128)(2,1)}, bf16[512,3072]{1,0:T(...) custom-call(bf16[512,768]{1,0:T(8,128)(2,1)} %bitcast.96, ...), custom_call_target="tpu_custom_call" | custom-call | flops 7247757312 | bytes 35651584 | tf_op jit(solution)/shard_map/ffn_fwd/pallas_call | solution.py:353
  84.0 16.9 %attn_fwd_1.1 = (bf16[2,256,768]{2,1,0:T(8,128)(2,1)}, bf16[2,12,256,256]{3,2,1,0:T(8,128)(2,1)}) custom-call(s32[2,1,256]{2,1,0:T(1,128)} %broadcast_in_dim.15.valid_ref, bf16[2,256,768]{2,1,0:T(8,128)(2,1)} %bitcast.75, bf16[2,256,768]{2,1,0:T(8,128)(2,1)} %bitcast.77, bf16[2,256,768]{2,1,0:T(8,128)(2,1)} %bitcast.79, bf16[2,256,768]{2,1,0:T(8,128)(2,1)} %bitcast.81, ...), custom_call_target="tpu_custom_call" | custom-call | flops 805306368 | bytes 12582912 | tf_op jit(solution)/shard_map/attn_fwd_1/pallas_call | solution.py:194
  100.9 30.9 %ffn_last.1 = (bf16[512,768]{1,0:T(8,128)(2,1)}, bf16[512,768]{1,0:T(8,128)(2,1)}, bf16[512,768]{1,0:T(8,128)(2,1)}, f32[512,768]{1,0:T(8,128)}, f32[8,768]{1,0:...) custom-call(s32[2]{0:T(128)} %pad_add_fusion.1.info_ref, ...), custom_call_target="tpu_custom_call" | custom-call | flops 15703474176 | bytes 31457280 | tf_op jit(solution)/shard_map/ffn_last/pallas_call | solution.py:514
  131.8 21.6 %attn_bwd_1.1 = (bf16[2,256,768]{2,1,0:T(8,128)(2,1)}, bf16[2,256,768]{2,1,0:T(8,128)(2,1)}, bf16[2,256,768]{2,1,0:T(8,128)(2,1)}, f32[512,768]{1,0:T(8,128)}, f32[8,768]{1,0:T(8,128)}) custom-call(bf16[2,12,256,256]{3,2,1,0:T(8,128)(2,1)} %get-tuple-element.86.p_ref, bf16[2,256,768]{2,1,0:T(8,128)(2,1)} %bitcast.76, bf16[2,256,768]{2,1,0:T(8,128)(2,1)} %bitcast.78, ...), custom_call_target="tpu_custom_call" | custom-call | flops 1811939328 | bytes 16777216 | tf_op jit(solution)/shard_map/attn_bwd_1/pallas_call | solution.py:281
  155.2 6.1 %first_back.1.dy_ref = f32[512,768]{1,0:T(8,128)} custom-call(f32[512,768]{1,0:T(8,128)} %get-tuple-element.85.dres_ref, bf16[512,768]{1,0:T(8,128)(2,1)} %bitcast.88, bf16[512,768]{1,0:T(8,128)(2,1)} %bitcast.90, bf16[512,768]{1,0:T(8,128)(2,1)} %bitcast.92, bf16[2,3,768,768]{3,2,1,0:T(8,128)(2,1)} %w_ref.5), custom_call_target="tpu_custom_call" | custom-call | flops 1811939328 | bytes 8388608 | tf_op jit(solution)/shard_map/first_back/pallas_call | solution.py:619
  161.3 27.0 %ffn_bwd.1 = (bf16[512,768]{1,0:T(8,128)(2,1)}, bf16[512,768]{1,0:T(8,128)(2,1)}, f32[512,768]{1,0:T(8,128)}, f32[8,768]{1,0:T(8,128)}, f32[8,3072]{1,0:T(8,128)...) custom-call(s32[2]{0:T(128)} %pad_add_fusion.1.info_ref, ...), custom_call_target="tpu_custom_call" | custom-call | flops 10267656192 | bytes 37748736 | tf_op jit(solution)/shard_map/ffn_bwd/pallas_call | solution.py:576
  188.3 29.9 %attn_bwd_2.1 = (bf16[2,256,768]{2,1,0:T(8,128)(2,1)}, bf16[2,512,768]{2,1,0:T(8,128)(2,1)}, bf16[2,512,768]{2,1,0:T(8,128)(2,1)}, f32[1024,768]{1,0:T(8,128)}, f32[8,768]{1,0:T(8,128)}) custom-call(bf16[2,12,256,512]{3,2,1,0:T(8,128)(2,1)} %get-tuple-element.99.p_ref, bf16[2,256,768]{2,1,0:T(8,128)(2,1)} %get-tuple-element.72.qw_ref, ...), custom_call_target="tpu_custom_call" | custom-call | flops 3623878656 | bytes 16777216 | tf_op jit(solution)/shard_map/attn_bwd_2/pallas_call | solution.py:281
  220.5 12.9 %qkv_grad.2 = (bf16[2304,384]{1,0:T(8,128)(2,1)}, bf16[2304,384]{1,0:T(8,128)(2,1)}, bf16[1536,384]{1,0:T(8,128)(2,1)}, bf16[1536,384]{1,0:T(8,128)(2,1)}) custom-call(s32[2]{0:T(128)} %pad_add_fusion.1.info_ref, bf16[512,768]{1,0:T(8,128)(2,1)} %bitcast.109, bf16[1024,768]{1,0:T(8,128)(2,1)} %bitcast.84, bf16[512,768]{1,0:T(8,128)(2,1)} %bitcast.99, ...), custom_call_target="tpu_custom_call" | custom-call | flops 4831838208 | bytes 16777216 | tf_op jit(solution)/shard_map/qkv_grad/pallas_call | solution.py:693
  233.5 9.7 %qkv_grad.3 = (bf16[2304,384]{1,0:T(8,128)(2,1)}, bf16[2304,384]{1,0:T(8,128)(2,1)}, bf16[1536,384]{1,0:T(8,128)(2,1)}, bf16[1536,384]{1,0:T(8,128)(2,1)}) custom-call(s32[2]{0:T(128)} %pad_add_fusion.1.info_ref, bf16[512,768]{1,0:T(8,128)(2,1)} %get-tuple-element.111.xq_ref.xk_ref, bf16[512,768]{1,0:T(8,128)(2,1)} %get-tuple-element.111.xq_ref.xk_ref, ...), custom_call_target="tpu_custom_call" | custom-call | flops 3019898880 | bytes 16777216 | tf_op jit(solution)/shard_map/qkv_grad/pallas_call | solution.py:693
  243.8 9.0 %tokens_back.1 = f32[2,512,768]{2,1,0:T(8,128)} custom-call(f32[2,256,768]{2,1,0:T(8,128)} %bitcast.85, bf16[2,256,768]{2,1,0:T(8,128)(2,1)} %get-tuple-element.101.dq_ref, bf16[2,512,768]{2,1,0:T(8,128)(2,1)} %get-tuple-element.102.dk_ref, bf16[2,512,768]{2,1,0:T(8,128)(2,1)} %get-tuple-element.103.dv_ref, bf16[2,3,768,768]{3,2,1,0:T(8,128)(2,1)} %w_ref.5), custom_call_target="tpu_custom_call" | custom-call | flops 3623878656 | bytes 14680064 | tf_op jit(solution)/shard_map/tokens_back/pallas_call | solution.py:642
  279.6 13.0 %collective-permute-done.11 = bf16[768,384]{1,0:T(8,128)(2,1)S(1)} collective-permute-done((bf16[768,384]{1,0:T(8,128)(2,1)S(1)}, bf16[768,384]{1,0:T(8,128)(2,1)S(1)}, u32[]{:S(2)}, u32[]{:S(2)}) %collective-permute-start.11) | collective-permute-done | bytes 589856 | tf_op jit(solution)/shard_map/ppermute | solution.py:713
  296.3 6.8 %collective-permute-done.23 = bf16[768,384]{1,0:T(8,128)(2,1)S(1)} collective-permute-done((bf16[768,384]{1,0:T(8,128)(2,1)S(1)}, bf16[768,384]{1,0:T(8,128)(2,1)S(1)}, u32[]{:S(2)}, u32[]{:S(2)}) %collective-permute-start.23) | collective-permute-done | bytes 589856 | tf_op jit(solution)/shard_map/ppermute | solution.py:713
  351.5 17.9 %collective-permute-done.17 = bf16[1152,384]{1,0:T(8,128)(2,1)S(1)} collective-permute-done((bf16[1152,384]{1,0:T(8,128)(2,1)S(1)}, bf16[1152,384]{1,0:T(8,128)(2,1)S(1)}, u32[]{:S(2)}, u32[]{:S(2)}) %collective-permute-start.17) | collective-permute-done | bytes 884768 | tf_op jit(solution)/shard_map/ppermute | solution.py:713
  383.0 9.0 %collective-permute-done.18 = bf16[576,384]{1,0:T(8,128)(2,1)S(1)} collective-permute-done((bf16[576,384]{1,0:T(8,128)(2,1)S(1)}, bf16[576,384]{1,0:T(8,128)(2,1)S(1)}, u32[]{:S(2)}, u32[]{:S(2)}) %collective-permute-start.18) | collective-permute-done | bytes 442400 | tf_op jit(solution)/shard_map/ppermute | solution.py:713
  392.4 6.7 %collective-permute-done.7 = bf16[288,384]{1,0:T(8,128)(2,1)S(1)} collective-permute-done((bf16[288,384]{1,0:T(8,128)(2,1)S(1)}, bf16[288,384]{1,0:T(8,128)(2,1)S(1)}, u32[]{:S(2)}, u32[]{:S(2)}) %collective-permute-start.7) | collective-permute-done | bytes 221216 | tf_op jit(solution)/shard_map/ppermute | solution.py:713
  399.2 6.0 %collective-permute-done.19 = bf16[288,384]{1,0:T(8,128)(2,1)S(1)} collective-permute-done((bf16[288,384]{1,0:T(8,128)(2,1)S(1)}, bf16[288,384]{1,0:T(8,128)(2,1)S(1)}, u32[]{:S(2)}, u32[]{:S(2)}) %collective-permute-start.19) | collective-permute-done | bytes 221216 | tf_op jit(solution)/shard_map/ppermute | solution.py:713
  405.4 5.9 %collective-permute-done.8 = bf16[144,384]{1,0:T(8,128)(2,1)S(1)} collective-permute-done((bf16[144,384]{1,0:T(8,128)(2,1)S(1)}, bf16[144,384]{1,0:T(8,128)(2,1)S(1)}, u32[]{:S(2)}, u32[]{:S(2)}) %collective-permute-start.8) | collective-permute-done | bytes 110624 | tf_op jit(solution)/shard_map/ppermute | solution.py:713
  411.3 5.7 %collective-permute-done.20 = bf16[144,384]{1,0:T(8,128)(2,1)S(1)} collective-permute-done((bf16[144,384]{1,0:T(8,128)(2,1)S(1)}, bf16[144,384]{1,0:T(8,128)(2,1)S(1)}, u32[]{:S(2)}, u32[]{:S(2)}) %collective-permute-start.20) | collective-permute-done | bytes 110624 | tf_op jit(solution)/shard_map/ppermute | solution.py:713
  424.4 18.1 %collective-permute-done.47 = bf16[1536,384]{1,0:T(8,128)(2,1)S(1)} collective-permute-done((bf16[1536,384]{1,0:T(8,128)(2,1)S(1)}, bf16[1536,384]{1,0:T(8,128)(2,1)S(1)}, u32[]{:S(2)}, u32[]{:S(2)}) %collective-permute-start.47) | collective-permute-done | bytes 1179680 | tf_op jit(solution)/shard_map/ppermute | solution.py:713
  449.6 10.3 %collective-permute-done.30 = bf16[768,384]{1,0:T(8,128)(2,1)S(1)} collective-permute-done((bf16[768,384]{1,0:T(8,128)(2,1)S(1)}, bf16[768,384]{1,0:T(8,128)(2,1)S(1)}, u32[]{:S(2)}, u32[]{:S(2)}) %collective-permute-start.30) | collective-permute-done | bytes 589856 | tf_op jit(solution)/shard_map/ppermute | solution.py:713
  472.9 7.3 %collective-permute-done.43 = bf16[384,384]{1,0:T(8,128)(2,1)S(1)} collective-permute-done((bf16[384,384]{1,0:T(8,128)(2,1)S(1)}, bf16[384,384]{1,0:T(8,128)(2,1)S(1)}, u32[]{:S(2)}, u32[]{:S(2)}) %collective-permute-start.43) | collective-permute-done | bytes 294944 | tf_op jit(solution)/shard_map/ppermute | solution.py:713
  (305 shorter events, 179.0 us)
Async XLA Ops:
  2.7 25.1 %collective-permute-start.1 = (bf16[2,128,768]{2,1,0:T(8,128)(2,1)}, bf16[2,128,768]{2,1,0:T(8,128)(2,1)}, u32[]{:S(2)}, u32[]{:S(2)}) collective-permute-start(bf16[2,128,768]{2,1,0:T(8,128)(2,1)} %get-tuple-element.137), channel_id=1, source_target_pairs={{0,1},{1,0},{2,3},{3,2},{4,5},{5,4},{6,7},{7,6},{8,9},{9,8},{10,11... | collective-permute-start | bytes 1179656 | tf_op jit(solution)/shard_map/ppermute | solution.py:713
  6.9 25.0 %collective-permute-start = (bf16[2,256,768]{2,1,0:T(8,128)(2,1)}, bf16[2,256,768]{2,1,0:T(8,128)(2,1)}, u32[]{:S(2)}, u32[]{:S(2)}) collective-permute-start(bf16[2,256,768]{2,1,0:T(8,128)(2,1)} %get-tuple-element.133), channel_id=1, source_target_pairs={{0,1},{1,0},{2,3},{3,2},{4,5},{5,4},{6,7},{7,6},{8,9},{9,8},{10,11... | collective-permute-start | bytes 2359304 | tf_op jit(solution)/shard_map/ppermute | solution.py:713
  155.1 97.7 %collective-permute-start.57 = (f32[12,768]{1,0:T(8,128)S(1)}, f32[12,768]{1,0:T(8,128)S(1)}, u32[]{:S(2)}, u32[]{:S(2)}) collective-permute-start(f32[12,768]{1,0:T(8,128)S(1)} %pad_maximum_fusion.6), channel_id=1, source_target_pairs={{0,2},{2,0},{4,6},{6,4},{8,10},{10,8},{12,14},{14,12},{16,18},{18,... | collective-permute-start | bytes 110600 | tf_op jit(solution)/shard_map/ppermute | solution.py:713
  220.0 34.7 %collective-permute-start.52 = (f32[12,768]{1,0:T(8,128)S(1)}, f32[12,768]{1,0:T(8,128)S(1)}, u32[]{:S(2)}, u32[]{:S(2)}) collective-permute-start(f32[12,768]{1,0:T(8,128)S(1)} %pad_maximum_fusion.5), channel_id=1, source_target_pairs={{0,2},{2,0},{4,6},{6,4},{8,10},{10,8},{12,14},{14,12},{16,18},{18,... | collective-permute-start | bytes 110600 | tf_op jit(solution)/shard_map/ppermute | solution.py:713
  233.4 40.6 %collective-permute-start.10 = (bf16[1536,384]{1,0:T(8,128)(2,1)}, bf16[1536,384]{1,0:T(8,128)(2,1)S(1)}, u32[]{:S(2)}, u32[]{:S(2)}) collective-permute-start(bf16[1536,384]{1,0:T(8,128)(2,1)} %get-tuple-element.110), channel_id=1, source_target_pairs={{0,2},{2,0},{4,6},{6,4},{8,10},{10,8},{12,14},{14,12},{16,18},{18,... | collective-permute-start | bytes 3538952 | tf_op jit(solution)/shard_map/ppermute | solution.py:713
  243.2 34.8 %collective-permute-start.22 = (bf16[1536,384]{1,0:T(8,128)(2,1)}, bf16[1536,384]{1,0:T(8,128)(2,1)S(1)}, u32[]{:S(2)}, u32[]{:S(2)}) collective-permute-start(bf16[1536,384]{1,0:T(8,128)(2,1)} %get-tuple-element.117), channel_id=1, source_target_pairs={{0,2},{2,0},{4,6},{6,4},{8,10},{10,8},{12,14},{14,12},{16,18},{18,... | collective-permute-start | bytes 3538952 | tf_op jit(solution)/shard_map/ppermute | solution.py:713
  252.8 53.3 %collective-permute-start.4 = (bf16[2304,384]{1,0:T(8,128)(2,1)S(1)}, bf16[2304,384]{1,0:T(8,128)(2,1)S(1)}, u32[]{:S(2)}, u32[]{:S(2)}) collective-permute-start(bf16[2304,384]{1,0:T(8,128)(2,1)S(1)} %copy-done.20), channel_id=1, source_target_pairs={{0,2},{2,0},{4,6},{6,4},{8,10},{10,8},{12,14},{14,12},{16,18},{18,... | collective-permute-start | bytes 5308424 | tf_op jit(solution)/shard_map/ppermute | solution.py:713
  269.0 67.5 %collective-permute-start.2 = (bf16[2,128,768]{2,1,0:T(8,128)(2,1)S(1)}, bf16[2,128,768]{2,1,0:T(8,128)(2,1)S(1)}, u32[]{:S(2)}, u32[]{:S(2)}) collective-permute-start(bf16[2,128,768]{2,1,0:T(8,128)(2,1)S(1)} %get-tuple-element.135), channel_id=1, source_target_pairs={{0,1},{1,0},{2,3},{3,2},{4,5},{5,4},{6,7},{7,6},{8,9},{9,8},{10,11... | collective-permute-start | bytes 1179656 | tf_op jit(solution)/shard_map/ppermute | solution.py:713
  274.0 65.2 %collective-permute-start.16 = (bf16[2304,384]{1,0:T(8,128)(2,1)S(1)}, bf16[2304,384]{1,0:T(8,128)(2,1)S(1)}, u32[]{:S(2)}, u32[]{:S(2)}) collective-permute-start(bf16[2304,384]{1,0:T(8,128)(2,1)S(1)} %copy-done.19), channel_id=1, source_target_pairs={{0,2},{2,0},{4,6},{6,4},{8,10},{10,8},{12,14},{14,12},{16,18},{18,... | collective-permute-start | bytes 5308424 | tf_op jit(solution)/shard_map/ppermute | solution.py:713
  278.4 24.6 %collective-permute-start.23 = (bf16[768,384]{1,0:T(8,128)(2,1)S(1)}, bf16[768,384]{1,0:T(8,128)(2,1)S(1)}, u32[]{:S(2)}, u32[]{:S(2)}) collective-permute-start(bf16[768,384]{1,0:T(8,128)(2,1)S(1)} %slice.440), channel_id=1, source_target_pairs={{0,1},{1,0},{2,3},{3,2},{4,5},{5,4},{6,7},{7,6},{8,9},{9,8},{10,11... | collective-permute-start | bytes 1769480 | tf_op jit(solution)/shard_map/ppermute | solution.py:713
  306.1 32.4 %collective-permute-start.3 = (bf16[2,256,768]{2,1,0:T(8,128)(2,1)S(1)}, bf16[2,256,768]{2,1,0:T(8,128)(2,1)S(1)}, u32[]{:S(2)}, u32[]{:S(2)}) collective-permute-start(bf16[2,256,768]{2,1,0:T(8,128)(2,1)S(1)} %dynamic-slice_convert_fusion), channel_id=1, source_target_pairs={{0,1},{1,0},{2,3},{3,2},{4,5},{5,4},{6,7},{7,6},{8,9},{9,8},{10,11... | collective-permute-start | bytes 2359304 | tf_op jit(solution)/shard_map/ppermute | solution.py:713
  309.6 60.3 %collective-permute-start.28 = (bf16[3072,384]{1,0:T(8,128)(2,1)S(1)}, bf16[3072,384]{1,0:T(8,128)(2,1)S(1)}, u32[]{:S(2)}, u32[]{:S(2)}) collective-permute-start(bf16[3072,384]{1,0:T(8,128)(2,1)S(1)} %copy-done.18), channel_id=1, source_target_pairs={{0,2},{2,0},{4,6},{6,4},{8,10},{10,8},{12,14},{14,12},{16,18},{18,... | collective-permute-start | bytes 7077896 | tf_op jit(solution)/shard_map/ppermute | solution.py:713
  339.3 33.1 %collective-permute-start.40 = (bf16[3072,384]{1,0:T(8,128)(2,1)S(1)}, bf16[3072,384]{1,0:T(8,128)(2,1)S(1)}, u32[]{:S(2)}, u32[]{:S(2)}) collective-permute-start(bf16[3072,384]{1,0:T(8,128)(2,1)S(1)} %copy-done.17), channel_id=1, source_target_pairs={{0,2},{2,0},{4,6},{6,4},{8,10},{10,8},{12,14},{14,12},{16,18},{18,... | collective-permute-start | bytes 7077896 | tf_op jit(solution)/shard_map/ppermute | solution.py:713
  340.9 33.8 %collective-permute-start.34 = (bf16[3072,384]{1,0:T(8,128)(2,1)S(1)}, bf16[3072,384]{1,0:T(8,128)(2,1)S(1)}, u32[]{:S(2)}, u32[]{:S(2)}) collective-permute-start(bf16[3072,384]{1,0:T(8,128)(2,1)S(1)} %copy-done.16), channel_id=1, source_target_pairs={{0,2},{2,0},{4,6},{6,4},{8,10},{10,8},{12,14},{14,12},{16,18},{18,... | collective-permute-start | bytes 7077896 | tf_op jit(solution)/shard_map/ppermute | solution.py:713
  342.9 34.1 %collective-permute-start.46 = (bf16[3072,384]{1,0:T(8,128)(2,1)S(1)}, bf16[3072,384]{1,0:T(8,128)(2,1)S(1)}, u32[]{:S(2)}, u32[]{:S(2)}) collective-permute-start(bf16[3072,384]{1,0:T(8,128)(2,1)S(1)} %copy-done.15), channel_id=1, source_target_pairs={{0,2},{2,0},{4,6},{6,4},{8,10},{10,8},{12,14},{14,12},{16,18},{18,... | collective-permute-start | bytes 7077896 | tf_op jit(solution)/shard_map/ppermute | solution.py:713
  372.4 46.9 %collective-permute-start.29 = (bf16[1536,384]{1,0:T(8,128)(2,1)S(1)}, bf16[1536,384]{1,0:T(8,128)(2,1)S(1)}, u32[]{:S(2)}, u32[]{:S(2)}) collective-permute-start(bf16[1536,384]{1,0:T(8,128)(2,1)S(1)} %slice.453), channel_id=1, source_target_pairs={{0,4},{2,6},{4,0},{6,2},{8,12},{10,14},{12,8},{14,10},{16,20},{18,... | collective-permute-start | bytes 3538952 | tf_op jit(solution)/shard_map/ppermute | solution.py:713
  374.7 44.9 %collective-permute-start.41 = (bf16[1536,384]{1,0:T(8,128)(2,1)S(1)}, bf16[1536,384]{1,0:T(8,128)(2,1)S(1)}, u32[]{:S(2)}, u32[]{:S(2)}) collective-permute-start(bf16[1536,384]{1,0:T(8,128)(2,1)S(1)} %slice.469), channel_id=1, source_target_pairs={{0,1},{1,0},{2,3},{3,2},{4,5},{5,4},{6,7},{7,6},{8,9},{9,8},{10,11... | collective-permute-start | bytes 3538952 | tf_op jit(solution)/shard_map/ppermute | solution.py:713
  377.0 46.9 %collective-permute-start.35 = (bf16[1536,384]{1,0:T(8,128)(2,1)S(1)}, bf16[1536,384]{1,0:T(8,128)(2,1)S(1)}, u32[]{:S(2)}, u32[]{:S(2)}) collective-permute-start(bf16[1536,384]{1,0:T(8,128)(2,1)S(1)} %slice.461), channel_id=1, source_target_pairs={{0,4},{2,6},{4,0},{6,2},{8,12},{10,14},{12,8},{14,10},{16,20},{18,... | collective-permute-start | bytes 3538952 | tf_op jit(solution)/shard_map/ppermute | solution.py:713
  382.5 60.0 %collective-permute-start.47 = (bf16[1536,384]{1,0:T(8,128)(2,1)S(1)}, bf16[1536,384]{1,0:T(8,128)(2,1)S(1)}, u32[]{:S(2)}, u32[]{:S(2)}) collective-permute-start(bf16[1536,384]{1,0:T(8,128)(2,1)S(1)} %slice.477), channel_id=1, source_target_pairs={{0,1},{1,0},{2,3},{3,2},{4,5},{5,4},{6,7},{7,6},{8,9},{9,8},{10,11... | collective-permute-start | bytes 3538952 | tf_op jit(solution)/shard_map/ppermute | solution.py:713
  417.0 27.9 %collective-permute-start.9 = (bf16[144,384]{1,0:T(8,128)(2,1)S(1)}, bf16[144,384]{1,0:T(8,128)(2,1)S(1)}, u32[]{:S(2)}, u32[]{:S(2)}) collective-permute-start(bf16[144,384]{1,0:T(8,128)(2,1)S(1)} %slice_add_fusion.29), channel_id=1, source_target_pairs={{0,1},{1,0},{2,3},{3,2},{4,5},{5,4},{6,7},{7,6},{8,9},{9,8},{10,11... | collective-permute-start | bytes 331784 | tf_op jit(solution)/shard_map/ppermute | solution.py:713
  419.3 28.0 %collective-permute-start.21 = (bf16[144,384]{1,0:T(8,128)(2,1)S(1)}, bf16[144,384]{1,0:T(8,128)(2,1)S(1)}, u32[]{:S(2)}, u32[]{:S(2)}) collective-permute-start(bf16[144,384]{1,0:T(8,128)(2,1)S(1)} %slice_add_fusion.28), channel_id=1, source_target_pairs={{0,1},{1,0},{2,3},{3,2},{4,5},{5,4},{6,7},{7,6},{8,9},{9,8},{10,11... | collective-permute-start | bytes 331784 | tf_op jit(solution)/shard_map/ppermute | solution.py:713
  419.6 40.3 %collective-permute-start.30 = (bf16[768,384]{1,0:T(8,128)(2,1)S(1)}, bf16[768,384]{1,0:T(8,128)(2,1)S(1)}, u32[]{:S(2)}, u32[]{:S(2)}) collective-permute-start(bf16[768,384]{1,0:T(8,128)(2,1)S(1)} %slice.455), channel_id=1, source_target_pairs={{0,1},{1,0},{2,3},{3,2},{4,5},{5,4},{6,7},{7,6},{8,9},{9,8},{10,11... | collective-permute-start | bytes 1769480 | tf_op jit(solution)/shard_map/ppermute | solution.py:713
  423.9 36.5 %collective-permute-start.42 = (bf16[768,384]{1,0:T(8,128)(2,1)S(1)}, bf16[768,384]{1,0:T(8,128)(2,1)S(1)}, u32[]{:S(2)}, u32[]{:S(2)}) collective-permute-start(bf16[768,384]{1,0:T(8,128)(2,1)S(1)} %slice.471), channel_id=1, source_target_pairs={{0,4},{2,6},{4,0},{6,2},{8,12},{10,14},{12,8},{14,10},{16,20},{18,... | collective-permute-start | bytes 1769480 | tf_op jit(solution)/shard_map/ppermute | solution.py:713
  442.5 24.9 %collective-permute-start.36 = (bf16[768,384]{1,0:T(8,128)(2,1)S(1)}, bf16[768,384]{1,0:T(8,128)(2,1)S(1)}, u32[]{:S(2)}, u32[]{:S(2)}) collective-permute-start(bf16[768,384]{1,0:T(8,128)(2,1)S(1)} %slice.463), channel_id=1, source_target_pairs={{0,1},{1,0},{2,3},{3,2},{4,5},{5,4},{6,7},{7,6},{8,9},{9,8},{10,11... | collective-permute-start | bytes 1769480 | tf_op jit(solution)/shard_map/ppermute | solution.py:713
  (60 other events, 655.3 us)

commit v2 on v0

v2 whole, which is shorter than its diff:
```python
import functools

import jax
import jax.numpy as jnp
from jax import lax
from jax.experimental import pallas as pl
from jax.experimental.pallas import tpu as pltpu
from jax.sharding import PartitionSpec as P

D = 768
HEADS = 12
HEAD_DIM = 64
FF = 3072
PANELS = FF // D
HALF = D // 2
EPS = 1e-06
MASKED = -1000000000.0
SCALE = HEAD_DIM ** (-0.5)
BF = jnp.bfloat16
F32 = jnp.float32
MIB = 1 << 20

SHARDS = 16
MESH = pl.DeviceIdType.MESH
UP_ROWS = PANELS * D // SHARDS
ROW = D // SHARDS
WIDE = 2
SMALL_ROWS = 12


def mm(a, b):
    return lax.dot_general(a, b, (((1,), (0,)), ((), ())), preferred_element_type=F32)


def mm_nt(a, b):
    return lax.dot_general(a, b, (((1,), (1,)), ((), ())), preferred_element_type=F32)


def mm_tn(a, b):
    return lax.dot_general(a, b, (((0,), (0,)), ((), ())), preferred_element_type=F32)


def ln_fwd(z):
    center = z - jnp.mean(z, axis=-1, keepdims=True)
    var = jnp.mean(center * center, axis=-1, keepdims=True)
    rstd = lax.rsqrt(var + EPS)
    return center * rstd, rstd


def ln_bwd(dy, xhat, rstd, gain):
    dx = dy * gain
    m1 = jnp.mean(dx, axis=-1, keepdims=True)
    m2 = jnp.mean(dx * xhat, axis=-1, keepdims=True)
    return rstd * (dx - m1 - xhat * m2)


GELU_K = 0.7978845608028654
GELU_C = 0.044715


def gelu_and_slope(z):
    z2 = z * z
    t = jnp.tanh(GELU_K * z * (1.0 + GELU_C * z2))
    half = 0.5 * (1.0 + t)
    slope = half + 0.5 * z * (1.0 - t * t) * (GELU_K * (1.0 + 3.0 * GELU_C * z2))
    return z * half, slope


def split_hi_lo(x):
    hi = x.astype(BF)
    return hi, (x - hi.astype(F32)).astype(BF)


def cost(flops, nbytes, trans=0):
    return pl.CostEstimate(flops=int(flops), bytes_accessed=int(nbytes), transcendentals=int(trans))


def params(limit=56, **kw):
    return pltpu.CompilerParams(vmem_limit_bytes=limit * MIB, **kw)


def full_spec(shape, memory_space=pltpu.VMEM):
    return pl.BlockSpec(memory_space=memory_space)


ANY = pl.BlockSpec(memory_space=pl.ANY)
VM = pl.BlockSpec(memory_space=pltpu.VMEM)
SM = pl.BlockSpec(memory_space=pltpu.SMEM)


def sds(shape, dtype):
    return jax.ShapeDtypeStruct(shape, dtype)


CORE = ("rows", 1)
ALONG_X = ("rows", 2)
ALONG_Y = ("seq", 1)
Z_NEAR = ("rows", 4)
Z_FAR = ("rows", 8)
Z_DIAG = ("rows", 12)
Z_ALL = ("rows", 0)
XZY = (CORE, ALONG_X, Z_NEAR, ALONG_Y, Z_FAR)
ZYX = (CORE, Z_NEAR, ALONG_Y, ALONG_X, Z_FAR)
XY = (CORE, ALONG_X, ALONG_Y, Z_ALL)
YX = (CORE, ALONG_Y, ALONG_X, Z_ALL)
BLOCK = 128
BLOCKS = D // (2 * BLOCK)


def bit(v, b):
    return lax.rem(lax.div(v, b), 2)


def partner(step):
    if isinstance(step[0], tuple):
        return {axis: spot for one in step for axis, spot in partner(one).items()}
    axis, b = step
    me = lax.axis_index(axis)
    spot = me
    for k in (1, 2, 4, 8):
        if b & k:
            spot = spot + k - 2 * k * bit(me, k)
    return {axis: spot}


def singles(step):
    return (Z_FAR, Z_NEAR, Z_DIAG) if step == Z_ALL else (step,)


def bits_of(order):
    return [one for step in order for one in ((Z_NEAR, Z_FAR) if step == Z_ALL else (step,))]


def greet(steps):
    steps = list(dict.fromkeys(one for step in steps for one in singles(step)))
    sem = pltpu.get_barrier_semaphore()
    for step in steps:
        pl.semaphore_signal(sem, inc=1, device_id=partner(step), device_id_type=MESH)
    pl.semaphore_wait(sem, len(steps))


def remote(src, dst, sems, i, step):
    return pltpu.make_async_remote_copy(
        src_ref=src,
        dst_ref=dst,
        send_sem=sems.at[i, 0],
        recv_sem=sems.at[i, 1],
        device_id=partner(step),
        device_id_type=MESH,
    )


def add_to(dst, m, b, bm, rows):
    blk = rows
    while blk * dst.shape[2] > 96 * HALF:
        blk //= 2

    def one(i, _):
        at = pl.ds(pl.multiple_of(i * blk, 16), blk)
        dst[m, at, :] = dst[m, at, :] + b[bm, at, :]
        return 0

    lax.fori_loop(0, rows // blk, one, 0)


class Kernel:
    def __init__(self):
        self.args, self.in_specs, self.out_specs, self.out_shape, self.scr = [], [], [], [], []

    def inp(self, x, spec=ANY):
        self.args.append(x)
        self.in_specs.append(spec)
        return ("i", len(self.args) - 1)

    def out(self, shape, dtype, spec=ANY):
        self.out_shape.append(sds(shape, dtype))
        self.out_specs.append(spec)
        return ("o", len(self.out_shape) - 1)

    def mem(self, shape, dtype=BF):
        self.scr.append(pltpu.VMEM(shape, dtype))
        return ("s", len(self.scr) - 1)

    def sems(self, *shape):
        self.scr.append(pltpu.SemaphoreType.DMA(shape))
        return ("s", len(self.scr) - 1)

    def run(self, body, name, cost_estimate, grid=(), cid=None, limit=56):
        n, m = len(self.args), len(self.out_shape)

        def kernel(*refs):
            groups = {"i": refs[:n], "o": refs[n : n + m], "s": refs[n + m :]}
            body(lambda handle: groups[handle[0]][handle[1]])

        kw = {} if cid is None else dict(collective_id=cid, has_side_effects=True)
        return pl.pallas_call(
            kernel,
            grid=grid,
            in_specs=self.in_specs,
            out_specs=self.out_specs,
            out_shape=self.out_shape,
            scratch_shapes=self.scr,
            compiler_params=params(limit, **kw),
            cost_estimate=cost_estimate,
            name=name,
        )(*self.args)


class Chain:
    def __init__(self, kn, whole, steps, close=False, born=None):
        self.steps, self.close, self.born, self.whole = steps, close, born is not None, whole
        j = len(steps)
        self.j = j
        if self.born:
            self.total, self.m, self.n, width = born
            self.arr = kn.mem((self.m, self.n, width))
        else:
            self.m, self.n, width = whole.shape
            self.src = kn.inp(whole)
            if j:
                self.total = kn.mem((self.m, self.n // (1 + len(singles(steps[0]))), width))
        m = self.m
        self.size = [self.n]
        for step in steps:
            self.size.append(self.size[-1] // (1 + len(singles(step))))
        self.land = [kn.mem((m * len(singles(s)), self.size[k + 1], width)) for k, s in enumerate(steps)]
        self.nf = self.size[-1]
        self.out = kn.out((m, self.nf, width), BF) if j else None
        self.other = kn.out((m, self.nf, width), BF) if close else None
        self.sem = kn.sems(2 * m + 3 * j + 3, 2)

    def bind(self, get):
        self.ref = get
        return self

    def core(self, i):
        g = self.ref
        return remote(g(self.total).at[i, pl.ds(self.n, self.n)], g(self.arr).at[i], g(self.sem), i, CORE)

    def sends(self, k, only=None):
        g, m, j = self.ref, self.m, self.j
        sem = g(self.sem)
        if k == j:
            mine = g(self.total).at[:, pl.ds(0, self.nf)] if j else g(self.src)
            return [remote(mine, g(self.other), sem, 2 * m + 3 * j, ALONG_Y)]
        n = self.size[k + 1]
        if self.born and k == 0:
            every = range(m) if only is None else [only]
            return [
                remote(g(self.total).at[i, pl.ds(n, n)], g(self.land[0]).at[i], sem, m + i, self.steps[0])
                for i in every
            ]
        source = g(self.total) if k or self.born else g(self.src)
        return [
            remote(
                source.at[:, pl.ds((i + 1) * n, n)], g(self.land[k]).at[pl.ds(i * m, m)], sem, 2 * m + 3 * k + i, one
            )
            for i, one in enumerate(singles(self.steps[k]))
        ]

    def fetch(self):
        g = self.ref
        return pltpu.make_async_copy(
            g(self.src).at[:, pl.ds(0, self.size[1])], g(self.total), g(self.sem).at[2 * self.m + 3 * self.j + 1, 0]
        )

    def keep(self):
        g = self.ref
        return pltpu.make_async_copy(
            g(self.total).at[:, pl.ds(0, self.nf)], g(self.out), g(self.sem).at[2 * self.m + 3 * self.j + 2, 0]
        )

    def first(self, i):
        g = self.ref
        self.core(i).wait()
        add_to(g(self.total), i, g(self.arr), i, self.n)
        for copy in self.sends(0, i):
            copy.start()

    def go(self, k):
        g = self.ref
        if k == 0 and self.j:
            self.fetch().start()
        if k > 0:
            if k == 1 and not self.born:
                self.fetch().wait()
            for copy in self.sends(k - 1):
                copy.wait()
            for b in range(len(singles(self.steps[k - 1]))):
                for i in range(self.m):
                    add_to(g(self.total), i, g(self.land[k - 1]), b * self.m + i, self.size[k])
        if k < self.j or self.close:
            for copy in self.sends(k):
                copy.start()
        if k == self.j and self.j:
            self.keep().start()

    def end(self):
        if self.close:
            for copy in self.sends(self.j):
                copy.wait()
        if self.j:
            self.keep().wait()

    def result(self, res):
        mine = res[self.out[1]] if self.j else self.whole
        return (mine, res[self.other[1]]) if self.close else mine


class Group:
    def __init__(self, kn, far, order, mats, rows_each, width=HALF):
        self.far, self.order, self.mats, self.rows = far, order, mats, rows_each
        self.n = SHARDS * rows_each
        self.buf = kn.mem((mats, 2 * self.n, width))
        if far:
            self.arr = kn.mem((mats, self.n, width))
        self.out = kn.out((mats, self.n if far else 2 * self.n, width), BF)
        self.sem = kn.sems(mats * SHARDS, 2)
        self.done = kn.sems(mats)

    def bind(self, get):
        self.ref = get
        self.sent = {i: [] for i in range(self.mats)}

    def locate(self):
        self.base = places(self.order, self.rows, self.far)

    def put(self, mat, tile, shards, first=0, pitch=None):
        put(self.ref(self.buf), mat, self.base, tile, shards, self.rows, first, pitch or self.rows)

    def leave(self, mat, start=0, n=None):
        if not self.far:
            return
        n = n or self.n
        self.sent[mat].append((start, n))
        self.copy(mat, len(self.sent[mat]) - 1).start()

    def copy(self, mat, i):
        g = self.ref
        start, n = self.sent[mat][i]
        source = g(self.buf).at[mat, pl.ds(self.n + start, n)]
        return remote(source, g(self.arr).at[mat, pl.ds(start, n)], g(self.sem), mat * SHARDS + i, CORE)

    def leave_shards(self, mat, first):
        if not self.far:
            return
        core = bit(lax.axis_index("rows"), 1)
        for x in range(2):
            for half in range(2):
                shard = first + 2 * x
                spot = jnp.where(core == 0, self.base[shard + 1, half], self.base[shard, half])
                self.leave(mat, pl.multiple_of(spot - self.n, 16), self.rows)

    def settle(self, mat):
        g = self.ref
        if self.far:
            for i in range(len(self.sent[mat])):
                self.copy(mat, i).wait()
            add_to(g(self.buf), mat, g(self.arr), mat, self.n)
        self.store(mat).start()

    def store(self, mat):
        g = self.ref
        n = self.n if self.far else 2 * self.n
        return pltpu.make_async_copy(g(self.buf).at[mat, pl.ds(0, n)], g(self.out).at[mat], g(self.done).at[mat])

    def end(self):
        for mat in range(self.mats):
            self.store(mat).wait()

    def result(self, res):
        return res[self.out[1]]


def pool_matrix(rows, cols):
    k = lax.broadcasted_iota(jnp.int32, (rows, cols), 0)
    t = lax.broadcasted_iota(jnp.int32, (rows, cols), 1)
    both = jnp.where((t == 2 * k) | (t == 2 * k - 1), 0.5, 0.0)
    return jnp.where((k == 0) & (t == 0), 1.0, both).astype(BF)


def pool_matrix_t(rows, cols):
    t = lax.broadcasted_iota(jnp.int32, (rows, cols), 0)
    k = lax.broadcasted_iota(jnp.int32, (rows, cols), 1)
    both = jnp.where((t == 2 * k) | (t == 2 * k - 1), 0.5, 0.0)
    return jnp.where((k == 0) & (t == 0), 1.0, both).astype(BF)


def head_masks():
    lane = lax.broadcasted_iota(jnp.int32, (1, 128), 1)
    first = jnp.where(lane < HEAD_DIM, 1.0, 0.0)
    return first.astype(BF), (1.0 - first).astype(BF)


def both_heads(x, masks):
    return jnp.concatenate([x * masks[0], x * masks[1]], axis=0)


QB = 128


def attn_fwd_step(stride, pairs, valid_ref, qw_ref, qr_ref, k_ref, v_ref, tab_ref, mixed_ref, inv_ref, p_ref):
    masks = head_masks()
    lane = lax.broadcasted_iota(jnp.int32, (1, 128), 1)
    keys = k_ref.shape[1]
    queries = qw_ref.shape[1]
    width = stride * QB + keys
    valid = valid_ref[0] > 0
    for pr in range(pairs):
        lanes = slice(pr * 128, (pr + 1) * 128)
        k = k_ref[0, :, lanes]
        v = jnp.concatenate([v_ref[0, :, lanes], jnp.ones((keys, 128), BF)], axis=1)
        outs = []
        for h in range(2):
            content = mm_nt(qw_ref[0, :, lanes] * (masks[h] * SCALE).astype(BF), k)
            relative = mm_nt(qr_ref[0, :, lanes] * (masks[h] * SCALE).astype(BF), tab_ref[:, lanes])
            parts = []
            for b in range(queries // QB):
                rows = slice(b * QB, (b + 1) * QB)
                t0 = stride * (queries - QB - b * QB)
                rolled = pltpu.roll(
                    relative[rows, t0 : t0 + width], width - stride * (QB - 1), 1, stride=stride, stride_axis=0
                )
                scores = jnp.where(valid, content[rows] + rolled[:, :keys], MASKED)
                terms = jnp.exp(scores - jnp.max(scores, axis=-1, keepdims=True)).astype(BF)
                p_ref[0, 2 * pr + h, rows, :] = terms
                parts.append(terms)
            outs.append(mm(jnp.concatenate(parts, axis=0), v))
        inv = 1.0 / jnp.where(lane < HEAD_DIM, outs[0][:, 128:], outs[1][:, 128:])
        inv_ref[0, :, lanes] = inv
        mixed_ref[0, :, lanes] = (jnp.where(lane < HEAD_DIM, outs[0][:, :128], outs[1][:, :128]) * inv).astype(BF)


def attn_fwd(stride, valid, qw, qr, k, v, tab, far=False, cid=None, extra=None):
    s, queries, _ = qw.shape
    keys = k.shape[1]
    table = tab.shape[0]
    pairs = 2
    steps = HEADS // 2 // pairs
    kn = Kernel()
    block = lambda n: pl.BlockSpec((1, n, 128 * pairs), lambda i, j: (i, 0, j))
    handles = [
        kn.inp(valid, pl.BlockSpec((1, 1, keys), lambda i, j: (i, 0, 0))),
        kn.inp(qw, block(queries)),
        kn.inp(qr, block(queries)),
        kn.inp(k, block(keys)),
        kn.inp(v, block(keys)),
        kn.inp(tab, pl.BlockSpec((table, 128 * pairs), lambda i, j: (0, j))),
        kn.out((s, queries, D), BF, block(queries)),
        kn.out((s, queries, D), F32, block(queries)),
        kn.out((s, HEADS, queries, keys), BF, pl.BlockSpec((1, 2 * pairs, queries, keys), lambda i, j: (i, j, 0, 0))),
    ]
    if extra is not None and far:
        part = extra.shape[1]
        h_ex, h_full, r_sem, l_sem = kn.inp(extra), kn.out((s, 2 * part, D), BF), kn.sems(1, 2), kn.sems(1)

    def body(get):
        if extra is not None and far:
            side = lax.axis_index("seq")
            here = get(h_full).at[:, pl.ds(side * part, part)]
            copies = lambda: (
                remote(get(h_ex).at[pl.ds((1 - side) * s, s)], here, get(r_sem), 0, ALONG_Y),
                pltpu.make_async_copy(get(h_ex).at[pl.ds(side * s, s)], here, get(l_sem).at[0]),
            )
            first = jnp.logical_and(pl.program_id(0) == 0, pl.program_id(1) == 0)
            end = jnp.logical_and(pl.program_id(0) == s - 1, pl.program_id(1) == steps - 1)

            @pl.when(first)
            def _():
                greet([ALONG_Y])
                for copy in copies():
                    copy.start()

        attn_fwd_step(stride, pairs, *[get(h) for h in handles])
        if extra is not None and far:

            @pl.when(end)
            def _():
                for copy in copies():
                    copy.wait()

    return kn.run(
        body,
        "attn_fwd_%d" % stride,
        cost(2 * s * HEADS * queries * keys * 64 * 4, 12 * MIB, s * HEADS * queries * keys),
        grid=(s, steps),
        cid=cid if extra is not None and far else None,
    )


def ffn_fwd(mixed, resid, w_out, w_up, w_down, w_qkv, attn_bias, up_bias, gain, nbias, obias):
    rows = mixed.shape[0]
    kn = Kernel()
    h_mixed, h_resid = kn.inp(mixed, VM), kn.inp(resid, VM)
    h_wout, h_up, h_down, h_qkv = (kn.inp(x) for x in (w_out, w_up, w_down, w_qkv))
    h_ab, h_upb, h_gain, h_nb, h_ob = (kn.inp(x, VM) for x in (attn_bias, up_bias, gain, nbias, obias))
    wout, wup, wdown, wqkv = kn.mem((D, D)), kn.mem((D, FF)), kn.mem((FF, D)), kn.mem((3, D, D))
    shapes = {"hid": (D, BF), "x1": (D, F32), "r1": (128, F32), "act": (FF, BF), "slope": (FF, BF), "x2": (D, F32)}
    shapes.update({"r2": (128, F32), "out": (D, F32), "low": (D, BF), "qw": (D, BF), "qr": (D, BF), "k": (D, BF), "v": (D, BF)})
    order = list(shapes)
    outs = {n: (kn.out((rows, c), t), kn.mem((rows, c), t)) for n, (c, t) in shapes.items()}
    l_sem, o_sem = kn.sems(4), kn.sems(len(order))
    h_total = kn.mem((rows, D), F32)

    def body(get):
        mem = lambda n: get(outs[n][1])
        store = lambda n: pltpu.make_async_copy(mem(n), get(outs[n][0]), get(o_sem).at[order.index(n)])
        pairs = ((get(h_wout).at[0], wout), (get(h_up).at[0], wup), (get(h_down).at[0], wdown), (get(h_qkv).at[1], wqkv))
        loads = [pltpu.make_async_copy(src, get(dst), get(l_sem).at[i]) for i, (src, dst) in enumerate(pairs)]
        for copy in loads:
            copy.start()
        gain_ref, nb_ref, ob_ref, ab_ref = get(h_gain), get(h_nb), get(h_ob), get(h_ab)
        loads[0].wait()
        x1, r1 = ln_fwd(get(h_resid)[...] + (mm(get(h_mixed)[...], get(wout)[...]) + ob_ref[0, 0:1, :]))
        mem("x1")[...] = x1
        mem("r1")[...] = jnp.broadcast_to(r1, (rows, 128))
        hidden = x1 * gain_ref[0, 0:1, :] + nb_ref[0, 0:1, :]
        mem("hid")[...] = hidden.astype(BF)
        for n in ("x1", "r1", "hid"):
            store(n).start()
        total = get(h_total)
        total[...] = hidden + ob_ref[0, 1:2, :]
        loads[1].wait()
        for c in range(0, PANELS, WIDE):
            cols = slice(c * D, (c + WIDE) * D)
            act, slope = gelu_and_slope(mm(mem("hid")[...], get(wup)[:, cols]) + get(h_upb)[0:1, cols])
            act = act.astype(BF)
            mem("act")[:, cols] = act
            mem("slope")[:, cols] = slope.astype(BF)
            if c == 0:
                loads[2].wait()
            total[...] += mm(act, get(wdown)[cols, :])
        store("act").start()
        store("slope").start()
        x2, r2 = ln_fwd(total[...])
        mem("x2")[...] = x2
        mem("r2")[...] = jnp.broadcast_to(r2, (rows, 128))
        out = x2 * gain_ref[0, 1:2, :] + nb_ref[0, 1:2, :]
        mem("out")[...] = out
        low = out.astype(BF)
        mem("low")[...] = low
        for n in ("x2", "r2", "out", "low"):
            store(n).start()
        loads[3].wait()
        q = mm(low, get(wqkv)[0])
        mem("qw")[...] = (q + ab_ref[1, 0:1, :]).astype(BF)
        mem("qr")[...] = (q + ab_ref[1, 1:2, :]).astype(BF)
        store("qw").start()
        store("qr").start()
        mem("k")[...] = mm(low, get(wqkv)[1]).astype(BF)
        store("k").start()
        mem("v")[...] = mm(low, get(wqkv)[2]).astype(BF)
        store("v").start()
        for n in order:
            store(n).wait()

    return kn.run(body, "ffn_fwd", cost(2 * rows * D * D * 12, 34 * MIB, rows * FF), limit=60)


def places(order, rows_each, far):
    me = lax.axis_index("rows") if far else 0
    side = lax.axis_index("seq") if far else 0
    base = {}
    for r in range(SHARDS):
        for half in range(2):
            spot = 0
            for axis, b in bits_of(order):
                c = half if axis == "seq" else (r // b) % 2
                mine = side if axis == "seq" else me
                spot = spot * 2 + (lax.rem(bit(mine, b) + c, 2) if far else c)
            base[r, half] = spot * rows_each
    return base


def put(buf_ref, mat, base, tile, shards, rows, first=0, pitch=None):
    low = tile.astype(BF)
    width = buf_ref.shape[2]
    for n, r in enumerate(shards):
        for half in range(2):
            start = base[r, half]
            if not isinstance(start, int):
                start = pl.multiple_of(start, 16)
            top = n * pitch + first
            buf_ref[mat, pl.ds(start, rows), :] = low[top : top + rows, half * width : (half + 1) * width]


NA = SHARDS * ROW
DOWN = 2
BORN_POINTS = ({1: 8, 2: 12}, {1: 12})
SMALL_STEPS = (
    (CORE,),
    (ALONG_X, ALONG_Y, (ALONG_X, ALONG_Y)),
    (Z_NEAR, Z_FAR, Z_DIAG),
)
FFN_ORDERS = ((XZY, YX, YX, ZYX, XY), (XZY, YX, YX, ZYX, ZYX))
ATT_ORDERS = (XY, YX)
DOWN_ROWS = UP_ROWS // DOWN


class FfnGrads:
    def __init__(self, kn, far, rows, layer):
        orders = FFN_ORDERS[layer]
        full = lambda shape: pl.BlockSpec(shape, lambda *g: (0,) * len(shape))
        self.dmixed = kn.out((rows, D), BF, full((rows, D)))
        self.dbranch = kn.out((rows, D), BF, full((rows, D)))
        self.dres = kn.out((rows, D), F32, full((rows, D)))
        self.small = kn.out((8, D), F32, full((8, D)))
        self.upg = kn.out((8, FF), F32, full((8, FF)))
        self.up = [Group(kn, far, orders[0], 3, ROW), Group(kn, far, orders[1], 1, ROW)]
        self.down = [Group(kn, far, order, 1, DOWN_ROWS) for order in orders[2:4]]
        self.outp = [Group(kn, far, orders[4], 1, ROW)]
        self.groups = self.up + self.down + self.outp
        self.wup, self.wdown = kn.mem((D, FF)), kn.mem((FF, D))
        self.act, self.slope = kn.mem((rows, FF)), kn.mem((rows, FF))
        self.dffn, self.dhid = kn.mem((rows, D)), kn.mem((rows, D), F32)
        self.near = kn.sems(4)

    def run(self, get, dy, x2, r2, gain2, gain1, wout_ref, hid_ref, mixed_ref, x1, r1, at):
        small_ref, upg_ref, dffn_ref, dhid_ref = get(self.small), get(self.upg), get(self.dffn), get(self.dhid)
        act, slope, wup, wdown = get(self.act), get(self.slope), get(self.wup), get(self.wdown)
        for group in self.groups:
            group.bind(get)
            group.locate()
        small_ref[...] = jnp.zeros_like(small_ref)
        dpost = ln_bwd(dy, x2, r2, gain2)
        small_ref[1:2, :] = jnp.sum(dy * x2, axis=0, keepdims=True)
        small_ref[3:4, :] = jnp.sum(dy, axis=0, keepdims=True)
        dffn = dpost.astype(BF)
        small_ref[5:6, :] = jnp.sum(dffn.astype(F32), axis=0, keepdims=True)
        dffn_ref[...] = dffn
        dhid_ref[...] = dpost
        at(0)
        each = SHARDS // PANELS
        for w in range(0, PANELS, WIDE):
            cols = slice(w * D, (w + WIDE) * D)
            dffn = dffn_ref[...]
            ddown = mm_tn(act[:, cols], dffn)
            shards = range(w * each, (w + WIDE) * each)
            for i, group in enumerate(self.down):
                group.put(0, ddown, shards, i * DOWN_ROWS, UP_ROWS)
                for p in range(w, w + WIDE):
                    group.leave_shards(0, p * each)
            dact = mm_nt(dffn, wdown[cols, :])
            dpre = (dact * slope[:, cols].astype(F32)).astype(BF)
            upg_ref[:, cols] = jnp.broadcast_to(jnp.sum(dpre.astype(F32), axis=0, keepdims=True), (8, WIDE * D))
            dup = mm_tn(hid_ref[...], dpre)
            for i in range(WIDE):
                group, mat = (self.up[0], w + i) if w + i < 3 else (self.up[1], 0)
                group.put(mat, dup[:, i * D : (i + 1) * D], range(SHARDS))
                group.leave(mat)
            dhid_ref[...] += mm_nt(dpre, wup[:, cols])
            if w + WIDE >= PANELS:
                self.up[0].settle(0)
                self.up[0].settle(1)
            at(w // WIDE + 1)
        dhid = dhid_ref[...]
        xh = x1()
        small_ref[0:1, :] = jnp.sum(dhid * xh, axis=0, keepdims=True)
        small_ref[2:3, :] = jnp.sum(dhid, axis=0, keepdims=True)
        dres = ln_bwd(dhid, xh, r1(), gain1)
        get(self.dres)[...] = dres
        dbranch = dres.astype(BF)
        get(self.dbranch)[...] = dbranch
        small_ref[4:5, :] = jnp.sum(dbranch.astype(F32), axis=0, keepdims=True)
        for group in self.outp:
            group.put(0, mm_tn(mixed_ref[...], dbranch), range(SHARDS))
            group.leave(0)
        get(self.dmixed)[...] = mm_nt(dbranch, wout_ref[0]).astype(BF)
        for group in self.down:
            group.settle(0)
        self.up[0].settle(2)
        self.up[1].settle(0)
        for group in self.outp:
            group.settle(0)
        for group in self.groups:
            group.end()

    def results(self, res):
        own = [res[h[1]] for h in (self.dmixed, self.dbranch, self.dres, self.small, self.upg)]
        return own, [group.result(res) for group in self.groups]


def ffn_last(far, cid, mixed, resid, cot, w_out, w_up, w_down, up_bias, gain, nbias, obias):
    rows = mixed.shape[0]
    kn = Kernel()
    whole = pl.BlockSpec((rows, D), lambda i: (0, 0))
    layer = pl.BlockSpec((1, 2, D), lambda i: (1, 0, 0))
    h_mixed, h_resid, h_cot = (kn.inp(x, whole) for x in (mixed, resid, cot))
    h_wout = kn.inp(w_out, pl.BlockSpec((1, D, D), lambda i: (1, 0, 0)))
    h_up, h_down = kn.inp(w_up), kn.inp(w_down)
    h_upb = kn.inp(up_bias, pl.BlockSpec((2, FF), lambda i: (0, 0)))
    h_gain, h_nbias, h_obias = (kn.inp(x, layer) for x in (gain, nbias, obias))
    h_lout = kn.out((rows, D), BF, whole)
    grads = FfnGrads(kn, far, rows, 1)
    h_hid, h_x1 = kn.mem((rows, D)), kn.mem((rows, D), F32)

    def body(get):
        if far:
            greet([CORE])
        near = get(grads.near)
        wup, wdown, act, slope, hid, x1s = (
            get(h) for h in (grads.wup, grads.wdown, grads.act, grads.slope, h_hid, h_x1)
        )
        dhid_s = get(grads.dhid)
        gain_ref, nbias_ref, obias_ref, upb_ref, wout_ref = (
            get(h) for h in (h_gain, h_nbias, h_obias, h_upb, h_wout)
        )
        cp_up = pltpu.make_async_copy(get(h_up).at[1], wup, near.at[0])
        cp_down = pltpu.make_async_copy(get(h_down).at[1], wdown, near.at[1])
        cp_up.start()
        cp_down.start()
        pre_norm = get(h_resid)[...] + (mm(get(h_mixed)[...], wout_ref[0]) + obias_ref[0, 0:1, :])
        x1, r1 = ln_fwd(pre_norm)
        x1s[...] = x1
        hidden = x1 * gain_ref[0, 0:1, :] + nbias_ref[0, 0:1, :]
        hid[...] = hidden.astype(BF)
        dhid_s[...] = hidden + obias_ref[0, 1:2, :]
        cp_up.wait()
        cp_down.wait()
        for c in range(0, PANELS, WIDE):
            cols = slice(c * D, (c + WIDE) * D)
            a, s = gelu_and_slope(mm(hid[...], wup[:, cols]) + upb_ref[1:2, cols])
            a = a.astype(BF)
            act[:, cols] = a
            slope[:, cols] = s.astype(BF)
            dhid_s[...] += mm(a, wdown[cols, :])
        x2, r2 = ln_fwd(dhid_s[...])
        get(h_lout)[...] = (x2 * gain_ref[0, 1:2, :] + nbias_ref[0, 1:2, :]).astype(BF)
        grads.run(
            get, get(h_cot)[...].astype(F32), x2, r2, gain_ref[0, 1:2, :], gain_ref[0, 0:1, :], wout_ref, hid,
            get(h_mixed), lambda: x1s[...], lambda: r1, lambda point: None,
        )

    res = kn.run(
        body, "ffn_last", cost(2 * rows * D * D * 26, 30 * MIB, rows * FF), grid=(1,), cid=cid if far else None, limit=63
    )
    return res[h_lout[1]], *grads.results(res)


def ffn_bwd(far, cid, chains, lout, dy, x2, r2, hid, mixed, x1, r1, gain, w_out, w_up, w_down, act, slope):
    rows = hid.shape[0]
    seqs, queries, _ = lout.shape
    kn = Kernel()
    whole = pl.BlockSpec((rows, D), lambda i: (0, 0))
    thin = pl.BlockSpec((rows, 128), lambda i: (0, 0))
    h_dy, h_x2, h_hid, h_mixed, h_x1 = (kn.inp(x, whole) for x in (dy, x2, hid, mixed, x1))
    h_r2, h_r1 = (kn.inp(x, thin) for x in (r2, r1))
    h_gain = kn.inp(gain, pl.BlockSpec((1, 2, D), lambda i: (0, 0, 0)))
    h_wout = kn.inp(w_out, pl.BlockSpec((1, D, D), lambda i: (0, 0, 0)))
    h_up, h_down, h_act, h_slope = (kn.inp(x) for x in (w_up, w_down, act, slope))
    grads = FfnGrads(kn, far, rows, 0)
    links = [Chain(kn, *c[:3]) for c in chains]
    if far:
        h_lout, h_got = kn.inp(lout), kn.out((seqs, queries // 2, D), BF)
        h_swap = kn.sems(1, 2)

    def body(get):
        near = get(grads.near)
        if far:
            greet([CORE, ALONG_X, ALONG_Y, Z_ALL])
            side = lax.axis_index("seq")
            swap_lout = remote(
                get(h_lout).at[:, pl.ds((1 - side) * (queries // 2), queries // 2)], get(h_got), get(h_swap), 0, ALONG_Y
            )
        for link in links:
            link.bind(get)
            link.go(0)
        loads = [
            pltpu.make_async_copy(get(h_act), get(grads.act), near.at[0]),
            pltpu.make_async_copy(get(h_down).at[0], get(grads.wdown), near.at[1]),
            pltpu.make_async_copy(get(h_slope), get(grads.slope), near.at[2]),
            pltpu.make_async_copy(get(h_up).at[0], get(grads.wup), near.at[3]),
        ]
        for copy in loads:
            copy.start()

        def at(point):
            if point == 0:
                for copy in loads:
                    copy.wait()
            for link, (_, _, _, when) in zip(links, chains):
                if point in when:
                    link.go(when[point])
            if far and point == 1:
                swap_lout.start()

        gain_ref = get(h_gain)
        grads.run(
            get, get(h_dy)[...], get(h_x2)[...], get(h_r2)[:, 0:1], gain_ref[0, 1:2, :], gain_ref[0, 0:1, :],
            get(h_wout), get(h_hid), get(h_mixed), lambda: get(h_x1)[...], lambda: get(h_r1)[:, 0:1], at,
        )
        for link, (_, _, close, _) in zip(links, chains):
            if not close:
                link.go(link.j)
        for link in links:
            link.end()
        if far:
            swap_lout.wait()

    res = kn.run(
        body, "ffn_bwd", cost(2 * rows * D * D * 18, 40 * MIB), grid=(1,), cid=cid if far else None, limit=63
    )
    return *grads.results(res), [link.result(res) for link in links], res[h_got[1]] if far else None


def attn_bwd_step(
    stride, seq, lanes, p_ref, inv_ref, qw_ref, qr_ref, k_ref, v_ref, tab_ref, dm_ref, dq, dk_out, dv_out, dtab, dbias
):
    masks = head_masks()
    lane = lax.broadcasted_iota(jnp.int32, (1, 128), 1)
    first = lane < HEAD_DIM
    keys = k_ref.shape[1]
    queries = qw_ref.shape[1]
    blocks = queries // QB
    width = stride * QB + keys
    flip_i = lax.broadcasted_iota(jnp.int32, (queries, queries), 0)
    flip_j = lax.broadcasted_iota(jnp.int32, (queries, queries), 1)
    flip = jnp.where(flip_i + flip_j == queries - 1, 1.0, 0.0).astype(BF)

    @pl.when(seq == 0)
    def _():
        dtab[:, lanes] = jnp.zeros((dtab.shape[0], 128), F32)
        dbias[:, lanes] = jnp.zeros((dbias.shape[0], 128), F32)

    k = k_ref[0]
    v = v_ref[0]
    inv = inv_ref[0]
    scaled = (dm_ref[0].astype(F32) * inv).astype(BF)
    qr_rev = mm(flip, qr_ref[0]).astype(BF)
    dk = jnp.zeros((keys, 128), F32)
    dv = jnp.zeros((keys, 128), F32)
    dqws, dqrs = [], []
    for h in range(2):
        dmh = scaled * masks[h]
        terms = p_ref[0, h]
        dprob = mm_nt(dmh, v)
        wide = terms.astype(F32)
        inner = jnp.sum(dprob * wide, axis=-1, keepdims=True) * inv[:, h * HEAD_DIM : h * HEAD_DIM + 1]
        ds = (wide * (dprob - inner)).astype(BF)
        dv = dv + mm_tn(terms, dmh)
        dk = dk + mm_tn(ds, qw_ref[0] * masks[h])
        dqws.append(mm(ds, k))
        rev = mm(flip, ds)
        back = []
        for b in range(blocks):
            rows = slice(b * QB, (b + 1) * QB)
            t0 = stride * b * QB
            padded = jnp.concatenate([rev[rows], jnp.zeros((QB, width - keys), F32)], axis=1)
            rel = pltpu.roll(padded, 0, 1, stride=stride, stride_axis=0).astype(BF)
            dtab[t0 : t0 + width, lanes] += mm_tn(rel, qr_rev[rows] * masks[h]) * SCALE
            back.append(mm(rel, tab_ref[t0 : t0 + width, :]))
        dqrs.append(jnp.concatenate(back, axis=0))
    dqw = jnp.where(first, dqws[0], dqws[1]) * SCALE
    hi, lo = split_hi_lo(jnp.where(first, dqrs[0], dqrs[1]))
    dqr = (mm(flip, hi) + mm(flip, lo)) * SCALE
    dq[pl.ds(pl.multiple_of(seq * queries, QB), queries), lanes] = (dqw + dqr).astype(BF)
    at = pl.ds(pl.multiple_of(seq * keys, QB), keys)
    dk_out[at, lanes] = (dk * SCALE).astype(BF)
    dv_out[at, lanes] = dv.astype(BF)
    dbias[0:1, lanes] += jnp.sum(dqw, axis=0, keepdims=True)
    dbias[1:2, lanes] += jnp.sum(dqr, axis=0, keepdims=True)


def back_layer(
    far, cid, layer, plan, p, inv, qw, qr, k, v, tab, dmixed, dres, w_qkv, xq, xk, enc, smalls=None
):
    s, queries, _ = qw.shape
    keys = k.shape[1]
    table = tab.shape[0]
    last = s * (HEADS // 2)
    nq, nk = s * queries, s * keys
    tail = smalls is not None
    kn = Kernel()
    seq_of = lambda g: lax.rem(jnp.minimum(g, last - 1), s)
    pair_of = lambda g: lax.div(jnp.minimum(g, last - 1), s)
    pair_block = lambda n: pl.BlockSpec((1, n, 128), lambda g: (seq_of(g), 0, pair_of(g)))
    h_p = kn.inp(p, pl.BlockSpec((1, 2, queries, keys), lambda g: (seq_of(g), pair_of(g), 0, 0)))
    h_inv, h_qw, h_qr, h_dm = (kn.inp(x, pair_block(queries)) for x in (inv, qw, qr, dmixed))
    h_k, h_v = (kn.inp(x, pair_block(keys)) for x in (k, v))
    h_tab = kn.inp(tab, pl.BlockSpec((table, 128), lambda g: (0, pair_of(g))))
    dq_s, dk_s, dv_s = kn.mem((nq, D)), kn.mem((nk, D)), kn.mem((nk, D))
    dtab_s, dbias_s = kn.mem((table, D), F32), kn.mem((8, D), F32)
    late = [(dres, F32), (xq, BF), (enc, BF)]
    if layer == 0 or xk is not xq:
        late.append((xk, BF))
    late_in = [kn.inp(x) for x, _ in late]
    late_mem = [kn.mem(x.shape, t) for x, t in late]
    h_w, h_wm = kn.inp(w_qkv), kn.mem((3, D, D))
    l_sem = kn.sems(len(late) + 1)
    chains = [Chain(kn, so_far, steps, close) for so_far, steps, close, _ in plan]
    whole = lambda shape: pl.BlockSpec(shape, lambda g: (0,) * len(shape))
    half = keys // 2
    born, groups = [], []
    for _ in range(BLOCKS):
        if tail and far:
            born += [Chain(kn, None, o[1:], True, (kn.mem((2, 2 * NA, BLOCK)), 2, NA, BLOCK)) for o in ATT_ORDERS]
        else:
            groups += [Group(kn, far, o, 2, ROW, BLOCK) for o in ATT_ORDERS]
    if tail and far:
        h_small = [kn.inp(x, whole(x.shape)) for x in smalls]
        sum_shape = (2 * SMALL_ROWS, D)
        h_sum = kn.out(sum_shape, F32, whole(sum_shape))
        sm = [kn.mem(sum_shape, F32) for _ in range(len(SMALL_STEPS))]
        sm_in = [kn.mem(sum_shape, F32) for step in SMALL_STEPS for _ in step]
        sm_sem = kn.sems(len(sm_in), 2)
        h_dx = kn.out((s, half, D), F32, whole((s, half, D)))
        h_piece, h_got, h_swap = kn.mem((s, half, D)), kn.out((s, half, D), BF), kn.sems(s, 2)
    else:
        h_dx = kn.out((nk, D), F32, whole((nk, D)))
        h_bias = kn.out((8, D), F32, whole((8, D)))
    greeted = [step for _, steps, _, _ in plan for step in steps] + [CORE]
    if tail:
        greeted = [CORE, ALONG_X, ALONG_Y, (ALONG_X, ALONG_Y), Z_ALL]

    def body(get):
        g = pl.program_id(0)
        dq, dk, dv, dtab, dbias = (get(h) for h in (dq_s, dk_s, dv_s, dtab_s, dbias_s))
        loads = [pltpu.make_async_copy(get(a), get(b), get(l_sem).at[i]) for i, (a, b) in enumerate(zip(late_in, late_mem))]
        loads.append(pltpu.make_async_copy(get(h_w).at[layer], get(h_wm), get(l_sem).at[len(late)]))
        for chain in chains + born:
            chain.bind(get)

        @pl.when(g == 0)
        def _():
            if far:
                greet(greeted)
            for copy in loads:
                copy.start()

        @pl.when(g < last)
        def _():
            lanes = pl.ds(pl.multiple_of(pair_of(g) * 128, 128), 128)
            attn_bwd_step(
                2 - layer, seq_of(g), lanes, get(h_p), get(h_inv), get(h_qw), get(h_qr), get(h_k), get(h_v), get(h_tab), get(h_dm),
                dq, dk, dv, dtab, dbias,
            )

        for point in range(last):
            acts = [(c, k) for c, (_, _, _, when) in zip(chains, plan) for k, w in when.items() if w == point]
            if acts:

                @pl.when(g == point)
                def _():
                    for chain, k in acts:
                        chain.go(k)

        dres_ref, xq_ref, enc_ref = (get(h) for h in late_mem[:3])
        xk_ref = get(late_mem[3]) if layer == 0 or xk is not xq else xq_ref
        for group in groups:
            group.bind(get)
        per = last // BLOCKS

        def swap_piece(i):
            return remote(get(h_piece).at[i], get(h_got).at[i], get(h_swap), i, ALONG_Y)

        def make(t):
            cols = slice(2 * t * BLOCK, 2 * (t + 1) * BLOCK)
            return (
                (1, 0, lambda: mm_tn(xk_ref[...], dv[:, cols])),
                (0, 0, lambda: mm_tn(xq_ref[...], dq[:, cols])),
                (1, 1, lambda: mm_tn(enc_ref[...], dtab[:, cols].astype(BF))),
                (0, 1, lambda: mm_tn(xk_ref[...], dk[:, cols])),
            )

        def gradients(t):
            bases = [places(order, ROW, far) for order in ATT_ORDERS]
            for group in groups:
                group.locate()
            for which, mat, tile in make(t):
                if tail and far:
                    chain = born[2 * t + which]
                    put(get(chain.total), mat, bases[which], tile(), range(SHARDS), ROW, 0, ROW)
                    chain.core(mat).start()
                else:
                    groups[2 * t + which].put(mat, tile(), range(SHARDS))
                    groups[2 * t + which].leave(mat)

        def settled(t):
            for which, mat, _ in make(t):
                if tail and far:
                    born[2 * t + which].first(mat)
                else:
                    groups[2 * t + which].settle(mat)

        for t in range(BLOCKS):

            @pl.when(g == (t + 1) * per - 1)
            def _():
                if t == 0:
                    for copy in loads:
                        copy.wait()
                gradients(t)

            if t < BLOCKS - 1:

                @pl.when(g == (t + 1) * per)
                def _():
                    settled(t)

                for chain in born[2 * t : 2 * t + 2]:
                    for k, point in BORN_POINTS[t].items():

                        @pl.when(g == point)
                        def _():
                            chain.go(k)

        @pl.when(g == last)
        def _():
            w = get(h_wm)
            dx_ref = get(h_dx)

            def at(point):
                for chain, (_, _, _, when) in zip(chains, plan):
                    for step, due in when.items():
                        if due == point:
                            chain.go(step)

            if tail and far:
                small_start(get, dbias)
            settled(BLOCKS - 1)
            if tail and far:
                small_round(get, 0)
            at(last)
            if layer == 1:
                dx_ref[...] = dres_ref[...] + (mm_nt(dq[...], w[0]) + mm_nt(dk[...], w[1]) + mm_nt(dv[...], w[2]))
            else:
                spread = pool_matrix_t(keys, queries)
                side = lax.axis_index("seq") if far else 0
                for i in range(s):
                    q_at, k_at = slice(i * queries, (i + 1) * queries), slice(i * keys, (i + 1) * keys)
                    hi, lo = split_hi_lo(dres_ref[q_at, :] + mm_nt(dq[q_at, :], w[0]))
                    dtok = mm_nt(dk[k_at, :], w[1]) + mm_nt(dv[k_at, :], w[2]) + (mm(spread, hi) + mm(spread, lo))
                    if tail and far:
                        low_half, high_half = dtok[:half], dtok[half:]
                        is_low = side == 0
                        dx_ref[i] = jnp.where(is_low, low_half, high_half)
                        get(h_piece)[i] = jnp.where(is_low, high_half, low_half).astype(BF)
                        swap_piece(i).start()
                    else:
                        dx_ref[k_at, :] = dtok
            at(last + 1)
            if tail and far:
                finish_tail(get, swap_piece)
                return
            get(h_bias)[...] = dbias[...]
            for chain in chains:
                chain.go(chain.j)
            for group in groups:
                group.end()
            for chain in chains:
                chain.end()

    def small_copies(get, k):
        top = sum(len(step) for step in SMALL_STEPS[:k])
        came = [get(h) for h in sm_in]
        return [
            (came[top + i], remote(get(sm[k]), came[top + i], get(sm_sem), top + i, one))
            for i, one in enumerate(SMALL_STEPS[k])
        ]

    def small_start(get, dbias):
        own = get(sm[0])
        small0, upg0, small1, upg1, bias1 = (get(h) for h in h_small)
        for top, small, upg, bias in ((0, small0, upg0, dbias), (SMALL_ROWS, small1, upg1, bias1)):
            own[top : top + 6, :] = small[0:6, :]
            own[top + 6 : top + 8, :] = bias[0:2, :]
            for p in range(PANELS):
                own[top + 8 + p : top + 9 + p, :] = upg[0:1, p * D : (p + 1) * D]
        for _, copy in small_copies(get, 0):
            copy.start()

    def small_round(get, k):
        pieces = small_copies(get, k)
        for _, copy in pieces:
            copy.wait()
        own = get(sm[k])
        dst = get(sm[k + 1]) if k + 1 < len(SMALL_STEPS) else get(h_sum)
        if len(pieces) == 1:
            dst[...] = own[...] + pieces[0][0][...]
        else:
            a, b, c = (ref[...] for ref, _ in pieces)
            dst[...] = (own[...] + a) + (b + c)
        if k + 1 < len(SMALL_STEPS):
            for _, copy in small_copies(get, k + 1):
                copy.start()

    def finish_tail(get, swap_piece):
        pending = {c: max(when) + 1 for c, (_, _, _, when) in zip(chains, plan)}
        for t in range(BLOCKS):
            for chain in born[2 * t : 2 * t + 2]:
                pending[chain] = max(BORN_POINTS[t]) + 1 if t < BLOCKS - 1 else 1
        order = born[2:4] + chains[:5] + born[4:] + born[:2] + chains[5:]
        for r in range(5):
            for chain in order:
                k = pending[chain]
                if k <= chain.j:
                    chain.go(k)
                    pending[chain] = k + 1
            if r + 1 < len(SMALL_STEPS):
                small_round(get, r + 1)
        for chain in order:
            chain.end()
        for i in range(s):
            swap_piece(i).wait()

    flops = 2 * s * HEADS * queries * keys * 64 * 9 + 2 * D * D * (4 * nq + 4 * nk + table)
    res = kn.run(
        body, "back_layer_%d" % layer, cost(flops, 40 * MIB), grid=(last + 1,), cid=cid if far else None, limit=62
    )
    moved = [chain.result(res) for chain in chains]
    if tail and far:
        return res[h_dx[1]], res[h_got[1]], res[h_sum[1]], moved, [chain.result(res) for chain in born]
    return res[h_dx[1]], res[h_bias[1]], moved, [group.result(res) for group in groups]


def steps_of(distances):
    half_width = D // 2
    frequency = 10000.0 ** (-jnp.arange(half_width, dtype=F32) / half_width)
    angles = distances.astype(F32)[:, None] * frequency[None, :]
    return jnp.stack([jnp.sin(angles), jnp.cos(angles)])


FINE = 32


def prologue(far, cid, tokens, w_qkv, w_pos, attn_bias):
    parts = 2 if far else 1
    s, part_len = tokens.shape[0] // parts, tokens.shape[1]
    length = part_len * parts
    queries = length // 2
    table = 2 * length
    coarse = steps_of(2 * (queries - 1) - FINE * jnp.arange(table // FINE, dtype=jnp.int32))
    fine = steps_of(-jnp.arange(FINE, dtype=jnp.int32))
    fine2 = steps_of(-2 * jnp.arange(FINE // 2, dtype=jnp.int32))
    kn = Kernel()
    h_tok, h_w, h_wp = (kn.inp(x) for x in (tokens, w_qkv, w_pos))
    h_coarse, h_fine, h_fine2, h_bias = (kn.inp(x, VM) for x in (coarse, fine, fine2, attn_bias))
    names = {}

    def result(name, shape, dtype=BF):
        names[name] = (kn.out(shape, dtype), kn.mem(shape, dtype))

    result("tok", (s, length, D))
    result("enc0", (table, D))
    result("enc1", (table // 2, D))
    result("tab0", (table, D))
    result("tab1", (table // 2, D))
    result("pooled", (s * queries, D), F32)
    for name in ("low", "qw", "qr"):
        result(name, (s * queries, D))
    for name in ("k", "v"):
        result(name, (s, length, D))
    h_wm, h_wpm = kn.mem((3, D, D)), kn.mem((2, D, D))
    o_sem, l_sem, r_sem = kn.sems(len(names)), kn.sems(3), kn.sems(1, 2)
    order = list(names)

    def body(get):
        mem = lambda name: get(names[name][1])

        def store(name):
            return pltpu.make_async_copy(mem(name), get(names[name][0]), get(o_sem).at[order.index(name)])

        ls = get(l_sem)
        tok = mem("tok")
        if far:
            side = lax.axis_index("seq")
            mine, other = pl.ds(side * s, s), pl.ds((1 - side) * s, s)
            greet([ALONG_Y])
            here = pl.ds(side * part_len, part_len)
            sends = [remote(get(h_tok).at[other], tok.at[:, here], get(r_sem), 0, ALONG_Y)]
            loads = [pltpu.make_async_copy(get(h_tok).at[mine], tok.at[:, here], ls.at[0])]
        else:
            sends = []
            loads = [pltpu.make_async_copy(get(h_tok), tok, ls.at[0])]
        loads += [
            pltpu.make_async_copy(get(h_wp), get(h_wpm), ls.at[1]),
            pltpu.make_async_copy(get(h_w).at[0], get(h_wm), ls.at[2]),
        ]
        for copy in sends + loads:
            copy.start()
        w = get(h_wm)

        def encode(dst, table_rows, fine_ref):
            n = fine_ref.shape[1]
            fs, fc = fine_ref[0], fine_ref[1]
            for a in range(table_rows // n):
                cs, cc = get(h_coarse)[0, a : a + 1, :], get(h_coarse)[1, a : a + 1, :]
                dst[a * n : (a + 1) * n, :HALF] = (cs * fc + cc * fs).astype(BF)
                dst[a * n : (a + 1) * n, HALF:] = (cc * fc - cs * fs).astype(BF)

        encode(mem("enc0"), table, get(h_fine))
        store("enc0").start()
        encode(mem("enc1"), table // 2, get(h_fine2))
        store("enc1").start()
        loads[1].wait()
        wp = get(h_wpm)
        mem("tab0")[...] = mm(mem("enc0")[...], wp[0]).astype(BF)
        store("tab0").start()
        mem("tab1")[...] = mm(mem("enc1")[...], wp[1]).astype(BF)
        store("tab1").start()
        for i in (0, 2):
            loads[i].wait()

        def keys_of(part):
            for i in range(s):
                x = tok[i, part, :]
                mem("k")[i, part, :] = mm(x, w[1]).astype(BF)
                mem("v")[i, part, :] = mm(x, w[2]).astype(BF)

        if far:
            keys_of(pl.ds(pl.multiple_of(side * part_len, part_len), part_len))
            for copy in sends:
                copy.wait()
            store("tok").start()
            keys_of(pl.ds(pl.multiple_of((1 - side) * part_len, part_len), part_len))
        else:
            store("tok").start()
            keys_of(pl.ds(0, length))
        store("k").start()
        store("v").start()
        gather = pool_matrix(queries, length)
        for i in range(s):
            at = slice(i * queries, (i + 1) * queries)
            pooled = mm(gather, tok[i])
            mem("pooled")[at, :] = pooled
            low = pooled.astype(BF)
            mem("low")[at, :] = low
            q = mm(low, w[0])
            mem("qw")[at, :] = (q + get(h_bias)[0, 0:1, :]).astype(BF)
            mem("qr")[at, :] = (q + get(h_bias)[0, 1:2, :]).astype(BF)
        for name in ("pooled", "low", "qw", "qr"):
            store(name).start()
        for name in order:
            store(name).wait()

    res = kn.run(
        body, "prologue", cost(2 * D * D * (3 * s * length + 2 * table), 30 * MIB), cid=cid if far else None
    )
    found = {name: res[h[0][1]] for name, h in names.items()}
    return found


def finish(done, sums, dtok, got, lout, lout_got):
    s, half, _ = dtok.shape
    q = lout_got.shape[1]
    names = [kind % (0, t) for t in range(BLOCKS) for kind in ("qk%d%d", "vp%d%d")]
    names += ["ua0", "ub0", "da0", "db0", "out0"]
    names += [kind % (1, t) for t in range(BLOCKS) for kind in ("qk%d%d", "vp%d%d")]
    names += ["ua1", "ub1", "da1", "db1", "out1"]
    kn = Kernel()
    hs = {n: (kn.inp(m, VM), kn.inp(o, VM)) for n, (m, o) in zip(names, done)}
    h_sum, h_dtok, h_got, h_lgot = (kn.inp(x, VM) for x in (sums, dtok, got, lout_got))
    h_lout = kn.inp(lout)
    o_lout = kn.out((2 * s, q, D), BF, VM)
    o_tok = kn.out((2 * s, half, D), F32, VM)
    o_qkv = kn.out((2, 3, ROW, D), F32, VM)
    o_out, o_pos = (kn.out((2, ROW, D), F32, VM) for _ in range(2))
    o_up = kn.out((2, ROW, FF), F32, VM)
    o_down = kn.out((2, UP_ROWS, D), F32, VM)
    o_attn = kn.out((2, 2, ROW), F32, VM)
    o_upb = kn.out((2, FF // SHARDS), F32, VM)
    o_gain, o_nb, o_ob = (kn.out((2, 2, ROW), F32, VM) for _ in range(3))
    h_lmem, h_sem = kn.mem((s, q, D)), kn.sems(1)

    def body(get):
        side, me = lax.axis_index("seq"), lax.axis_index("rows")
        copy = pltpu.make_async_copy(
            get(h_lout).at[:, pl.ds(pl.multiple_of(side * q, q), q)], get(h_lmem), get(h_sem).at[0]
        )
        copy.start()
        mine, other = pl.ds(side * s, s), pl.ds((1 - side) * s, s)
        get(o_tok)[mine] = get(h_dtok)[...]
        get(o_tok)[other] = get(h_got)[...].astype(F32)
        get(o_lout)[other] = get(h_lgot)[...]

        def halves(name, mat, dst, lead, base=0, rows=slice(None)):
            for h, which in zip(hs[name], (side, 1 - side)):
                width = get(h).shape[2]
                lanes = pl.ds(pl.multiple_of(base + which * width, 128), width)
                dst[(*lead, rows, lanes)] = get(h)[mat].astype(F32)

        for l in range(2):
            at = lambda name: "%s%d" % (name, l)
            for t in range(BLOCKS):
                for i, (kind, mat) in enumerate((("qk", 0), ("qk", 1), ("vp", 0))):
                    halves("%s%d%d" % (kind, l, t), mat, get(o_qkv), (l, i), 2 * t * BLOCK)
                halves("vp%d%d" % (l, t), 1, get(o_pos), (l,), 2 * t * BLOCK)
            halves(at("out"), 0, get(o_out), (l,))
            for p in range(PANELS):
                halves(at("ua") if p < 3 else at("ub"), p % 3, get(o_up), (l,), p * D)
            for i, name in enumerate(("da", "db")):
                halves(at(name), 0, get(o_down), (l,), rows=slice(i * DOWN_ROWS, (i + 1) * DOWN_ROWS))
        both = get(h_sum)[...]
        turned = pltpu.roll(both, lax.rem(D - me * ROW, D), 1)
        for l in range(2):
            r = 12 * l
            for o, row in ((o_gain, 0), (o_nb, 2), (o_ob, 4), (o_attn, 6)):
                get(o)[l] = turned[r + row : r + row + 2, :ROW]
        wide = FF // SHARDS
        per = D // wide
        shifted = pltpu.roll(both, lax.rem(D - lax.rem(me, per) * wide, D), 1)
        for l in range(2):
            picked = jnp.zeros((1, D), F32)
            for p in range(PANELS):
                picked = picked + jnp.where(lax.div(me, per) == p, shifted[12 * l + 8 + p : 12 * l + 9 + p, :], 0.0)
            get(o_upb)[l : l + 1, :] = picked[:, :wide]
        copy.wait()
        get(o_lout)[mine] = get(h_lmem)[...]

    return tuple(kn.run(body, "finish", cost(1e6, 16 * MIB)))


def swap(x, axis, b):
    n = lax.axis_size(axis)
    return lax.ppermute(x, axis, [(i, i ^ b) for i in range(n)])


def natural(both, order, rows_each):
    mats = both.shape[0]
    both = both.reshape(mats, 2, 2, 2, 2, 2, rows_each, both.shape[-1])
    at = {step: 1 + i for i, step in enumerate(bits_of(order))}
    return both.transpose(0, at[Z_FAR], at[Z_NEAR], at[ALONG_X], at[CORE], 6, at[ALONG_Y], 7)


def to_sequences(x, side, parts):
    own = x.shape[0] // parts
    mine = lax.dynamic_slice_in_dim(x, side * own, own, 0)
    other = swap(lax.dynamic_slice_in_dim(x, (1 - side) * own, own, 0), "seq", 1)
    return jnp.where(
        side == 0, jnp.concatenate([mine, other], axis=1), jnp.concatenate([other, mine], axis=1)
    )


def to_positions(x, side, parts, wire):
    own = x.shape[1] // parts
    mine = lax.dynamic_slice_in_dim(x, side * own, own, 1)
    other = swap(lax.dynamic_slice_in_dim(x, (1 - side) * own, own, 1).astype(wire), "seq", 1).astype(x.dtype)
    return jnp.where(
        side == 0, jnp.concatenate([mine, other], axis=0), jnp.concatenate([other, mine], axis=0)
    )


def elsewhere(att0, ffn0, att1, ffn1, smalls, n_rows, me):
    flat = lambda x: x.reshape(x.shape[0], -1, x.shape[-1] * x.shape[-2])
    rows = lambda x, order: flat(natural(x, order, ROW))
    total = lambda x: lax.psum(lax.psum_scatter(x, "rows", scatter_dimension=1, tiled=True).astype(F32), "seq")

    def down(a, b):
        parts = [natural(x, order, DOWN_ROWS) for x, order in zip((a, b), FFN_ORDERS[0][2:4])]
        return flat(jnp.concatenate(parts, axis=5))

    def att(x):
        both = [jnp.concatenate([rows(b, o) for b, o in zip(x[2 * t : 2 * t + 2], ATT_ORDERS)]) for t in range(BLOCKS)]
        return total(jnp.concatenate(both, axis=2))

    att0, att1 = att(att0), att(att1)
    outs = [total(rows(f[4], FFN_ORDERS[l][4])) for l, f in enumerate((ffn0, ffn1))]
    ups = [total(jnp.concatenate([rows(x, o) for x, o in zip(f[:2], FFN_ORDERS[0])])) for f in (ffn0, ffn1)]
    downs = [total(down(f[2], f[3])) for f in (ffn0, ffn1)]
    sums = lax.psum(smalls, ("rows", "seq")).reshape(2, -1, D)
    own = D // n_rows
    cut = lambda x: lax.dynamic_slice_in_dim(x, me * own, own, 2)
    upb = lax.dynamic_slice_in_dim(sums[:, 8:].reshape(2, FF), me * (FF // n_rows), FF // n_rows, 1)
    panels = lambda x: jnp.concatenate(list(x), axis=1)
    return (
        jnp.stack([att0[:3], att1[:3]]),
        jnp.concatenate(outs),
        jnp.stack([att0[3], att1[3]]),
        jnp.stack([panels(x) for x in ups]),
        jnp.concatenate(downs),
        cut(sums[:, 6:8]),
        upb,
        cut(sums[:, 0:2]),
        cut(sums[:, 2:4]),
        cut(sums[:, 4:6]),
    )


def on_device(
    tokens, lengths, key_mask, cotangent, w_qkv, w_out, w_pos, w_up, w_down, attn_bias, up_bias, norm_gain,
    norm_bias, out_bias,
):
    side = lax.axis_index("seq")
    parts = lax.axis_size("seq")
    n_rows = lax.axis_size("rows")
    me = lax.axis_index("rows")
    far = n_rows == SHARDS and parts == 2
    seqs = tokens.shape[0] // parts
    length = tokens.shape[1] * parts
    queries = length // 2
    mine = lambda x: lax.dynamic_slice_in_dim(x, side * seqs, seqs, 0)
    spots = jnp.arange(length, dtype=jnp.int32)[None, :]
    key_valid = jnp.where(spots < mine(lengths)[:, None], mine(key_mask), 0)
    shifted_valid = jnp.concatenate([key_valid[:, :1], key_valid[:, :-1]], axis=1)
    pooled_valid = jnp.max(shifted_valid.reshape(seqs, queries, 2), axis=2)
    flat = lambda x: x.reshape(-1, x.shape[-1])
    sets = lambda x: x.reshape(seqs, -1, D)

    if not far:
        tokens, cotangent = to_sequences(tokens, side, parts), to_sequences(cotangent, side, parts)
    start = prologue(far, 1, tokens, w_qkv, w_pos, attn_bias)
    tab0, tab1, enc0, enc1 = (start[n] for n in ("tab0", "tab1", "enc0", "enc1"))
    qw0, qr0, k0, v0 = sets(start["qw"]), sets(start["qr"]), start["k"], start["v"]
    mixed0, inv0, p0, *swapped = attn_fwd(2, key_valid[:, None, :], qw0, qr0, k0, v0, tab0, far, 6, cotangent)
    cot = swapped[0] if far else cotangent
    mixed0 = flat(mixed0)
    hid, x1, r1, act, slope, x2, r2, first, first_low, qw1, qr1, k1, v1 = ffn_fwd(
        mixed0, start["pooled"], w_out, w_up, w_down, w_qkv, attn_bias, up_bias, norm_gain, norm_bias, out_bias
    )
    qw1, qr1, k1, v1 = sets(qw1), sets(qr1), sets(k1), sets(v1)
    mixed1, inv1, p1 = attn_fwd(1, pooled_valid[:, None, :], qw1, qr1, k1, v1, tab1)
    mixed1 = flat(mixed1)
    lout, (dmixed1, dbranch1, dres1, small1, upg1), ffn1 = ffn_last(
        far, 2, mixed1, first, flat(cot), w_out, w_up, w_down, up_bias, norm_gain, norm_bias, out_bias
    )
    lout = sets(lout)
    plan = []
    if far:
        plan = [(x, order[1:3], False, {0: 0, 1: 9}) for x, order in zip(ffn1, FFN_ORDERS[1])]
    dfirst, dbias1, moved, att1 = back_layer(
        far, 3, 1, plan, p1, inv1, qw1, qr1, k1, v1, tab1, sets(dmixed1), dres1, w_qkv, first_low, first_low, enc1,
    )
    chains = []
    if far:
        for x, order in zip(moved, FFN_ORDERS[1]):
            steps = order[3:]
            chains.append((x, steps, True, {k: k for k in range(1, len(steps) + 1)}))
        chains += [(x, order[1:3], False, {2: 1}) for x, order in zip(att1, ATT_ORDERS * BLOCKS)]
    (dmixed0, dbranch0, dres0, small0, upg0), ffn0, moved, lout_got = ffn_bwd(
        far, 4, chains, lout, dfirst, x2, r2, hid, mixed0, x1, r1, norm_gain, w_out, w_up, w_down, act, slope
    )
    plan = []
    if far:
        late = {0: 0, 1: 8, 2: 11}
        when = ({0: 0, 1: 7, 2: 11}, {0: 0, 1: 7, 2: 11}, {0: 0, 1: 7, 2: 11}, {0: 0, 1: 7, 2: 11}, late)
        plan = [(x, order[1:], True, due) for x, order, due in zip(ffn0, FFN_ORDERS[0], when)]
        plan += [(x, order[3:], True, {0: 8}) for x, order in zip(moved[5:], ATT_ORDERS * BLOCKS)]
    args = (p0, inv0, qw0, qr0, k0, v0, tab0, sets(dmixed0), dres0, w_qkv, start["low"], flat(start["tok"]), enc0)
    if far:
        dtok, got, sums, ended, att0 = back_layer(far, 5, 0, plan, *args, smalls=(small0, upg0, small1, upg1, dbias1))
        done = att0 + ended + moved[:5]
        return finish(done, sums, dtok, got, lout, lout_got)
    dtok, dbias0, _, att0 = back_layer(far, 5, 0, plan, *args)
    small = lambda s, u, b: jnp.concatenate([s[:6], b[:2], u[0].reshape(PANELS, D)], axis=0)
    smalls = jnp.concatenate([small(small0, upg0, dbias0), small(small1, upg1, dbias1)], axis=0)
    return (
        to_positions(lout, side, parts, BF),
        to_positions(sets(dtok), side, parts, BF),
        *elsewhere(att0, ffn0, att1, ffn1, smalls, n_rows, me),
    )


def solution(mesh):
    seq3 = P("rows", "seq", None)
    in_specs = (seq3, P("rows"), P("rows", None), seq3) + (P(),) * 10
    mat = P(None, "rows", None)
    vec = P(None, None, "rows")
    out_specs = (seq3, seq3, P(None, None, "rows", None), mat, mat, mat, mat, vec, P(None, "rows"), vec, vec, vec)
    return jax.shard_map(on_device, mesh=mesh, in_specs=in_specs, out_specs=out_specs, check_vma=False)
```

time: 1460 us -> 344 us (0.24)
  waiting for transfers between devices: 695 us -> 0 us
  Pallas kernels: 0 us -> 331 us
  local copies, waits for them, and re-layouts: 310 us -> 2.12 us
  matrix products: 233 us -> 0 us
  blocking collectives: 95.5 us -> 0 us
  other arithmetic: 90.1 us -> 2.92 us
  between operations: 16.7 us -> 0.95 us
    reduce_scatter x9 -> x0, waiting for transfers between devices: 694 us -> none  [the longest x1 200 us: on_device(): lax.psum_scatter(grad_up, ('rows', 'seq'), scatter_dimension=1, tiled=True)]
    pallas_call x0 -> x9, Pallas kernels: none -> 331 us  [run(): pl.pallas_call(kernel, grid=grid, in_specs=self.in_specs, out_specs=self....]
    dot_general x58 -> x0, matrix products: 233 us -> none  [the longest x42 177 us: contract(): jnp.einsum(pattern, left_side, right_side, preferred_element_type=jnp.flo...]
    reshape x21 -> x1, local copies, waits for them, and re-layouts: 159 us -> 0.2 us  [on_device(): pooled_valid = jnp.max(shifted_valid.reshape(seqs, queries, 2), axis=2)]
    all_gather x10 -> x0, blocking collectives: 55.4 us -> none  [the longest x1 8.24 us: on_device(): lax.all_gather(sum_down.astype(jnp.bfloat16), 'seq', axis=1, tiled=True)]
    another operation x22 -> x2, other arithmetic: 46.8 us -> 1.32 us  [steps_of(): return jnp.stack([jnp.sin(angles), jnp.cos(angles)])]
    unnamed x1 -> x0, blocking collectives: 40.1 us -> none
    slice x9 -> x1, local copies, waits for them, and re-layouts: 36.8 us -> 0.01 us  [on_device(): key_valid[:, :1]]
  transfers between devices with their start and end apart: 16 -> 0, of which waited for: 5 -> 0; matrix products, arithmetic and copies ran while one was open for 35% -> 0% of each run, Pallas kernels for 0% -> 0%
where the time goes in v2:
time: 344 us; the launch traced here: 337 us
  Pallas kernels  331 us (96%)
    pallas_call x9, Pallas kernels, run(): pl.pallas_call(kernel, grid=grid, in_specs=self.in_specs, out_specs=self....  331 us

profile of v2, /device:TPU:0, one launch (start us, length us, event | category | flops | bytes accessed | tf_op | source)
XLA Modules:
  0.0 337.4 jit_solution(735752200532332753)
XLA Ops:
  0.6 0.7 dynamic_slice.6
  1.4 0.8 compare_select_fusion
  2.2 0.1 pad_add_fusion
  2.3 0.6 broadcast_in_dim.9.refs_0_
  2.9 0.2 multiply_sine_fusion.2
  3.0 0.6 pad_maximum_fusion.2.refs_5_
  3.7 0.4 multiply_sine_fusion
  4.1 0.7 pad_maximum_fusion
  4.8 0.2 reshape.358
  5.0 0.1 reduce_max.9
  5.1 0.6 broadcast_in_dim.10.refs_0_
  5.7 25.9 %prologue.1 = (bf16[2,512,768]{2,1,0:T(8,128)(2,1)}, bf16[1024,768]{1,0:T(8,128)(2,1)}, bf16[512,768]{1,0:T(8,128)(2,1)}, bf16[1024,768]{1,0:T(8,128)(2,1)}, bf1...) custom-call(bf16[4,256,768]{2,1,0:T(8,128)(2,1)} %refs_0_.1, ...), custom_call_target="tpu_custom_call" | custom-call | flops 6039797760 | bytes 31457280 | tf_op jit(solution)/shard_map/prologue/pallas_call | solution.py:196
  31.6 19.4 %attn_fwd_2.1 = (bf16[2,256,768]{2,1,0:T(8,128)(2,1)}, f32[2,256,768]{2,1,0:T(8,128)}, bf16[2,12,256,512]{3,2,1,0:T(8,128)(2,1)}, bf16[2,256,768]{2,1,0:T(8,128)(2,1)}) custom-call(s32[2,1,512]{2,1,0:T(1,128)} %broadcast_in_dim.9.refs_0_, bf16[2,256,768]{2,1,0:T(8,128)(2,1)} %bitcast.14, bf16[2,256,768]{2,1,0:T(8,128)(2,1)} %bitcast.16, ...), custom_call_target="tpu_custom_call" | custom-call | flops 1610612736 | bytes 12582912 | tf_op jit(solution)/shard_map/attn_fwd_2/pallas_call | solution.py:196
  51.0 16.6 %ffn_fwd.1 = (bf16[512,768]{1,0:T(8,128)(2,1)}, f32[512,768]{1,0:T(8,128)}, f32[512,128]{1,0:T(8,128)}, bf16[512,3072]{1,0:T(8,128)(2,1)}, bf16[512,3072]{1,0:T(...) custom-call(bf16[512,768]{1,0:T(8,128)(2,1)} %bitcast.28, ...), custom_call_target="tpu_custom_call" | custom-call | flops 7247757312 | bytes 35651584 | tf_op jit(solution)/shard_map/ffn_fwd/pallas_call | solution.py:196
  67.6 13.6 %attn_fwd_1.1 = (bf16[2,256,768]{2,1,0:T(8,128)(2,1)}, f32[2,256,768]{2,1,0:T(8,128)}, bf16[2,12,256,256]{3,2,1,0:T(8,128)(2,1)}) custom-call(s32[2,1,256]{2,1,0:T(1,128)} %broadcast_in_dim.10.refs_0_, bf16[2,256,768]{2,1,0:T(8,128)(2,1)} %bitcast.18, bf16[2,256,768]{2,1,0:T(8,128)(2,1)} %bitcast.20, bf16[2,256,768]{2,1,0:T(8,128)(2,1)} %bitcast.22, ...), custom_call_target="tpu_custom_call" | custom-call | flops 805306368 | bytes 12582912 | tf_op jit(solution)/shard_map/attn_fwd_1/pallas_call | solution.py:196
  81.2 34.8 %ffn_last.1 = (bf16[512,768]{1,0:T(8,128)(2,1)}, bf16[512,768]{1,0:T(8,128)(2,1)}, bf16[512,768]{1,0:T(8,128)(2,1)}, f32[512,768]{1,0:T(8,128)}, f32[8,768]{1,0:...) custom-call(bf16[512,768]{1,0:T(8,128)(2,1)} %bitcast.32, ...), custom_call_target="tpu_custom_call" | custom-call | flops 15703474176 | bytes 31457280 | tf_op jit(solution)/shard_map/ffn_last/pallas_call | solution.py:196
  116.0 47.7 %back_layer_1.1 = (bf16[3,192,384]{2,1,0:T(8,128)(2,1)}, bf16[1,192,384]{2,1,0:T(8,128)(2,1)}, bf16[1,384,384]{2,1,0:T(8,128)(2,1)}, bf16[1,384,384]{2,1,0:T(8,1...) custom-call(bf16[2,12,256,256]{3,2,1,0:T(8,128)(2,1)} %get-tuple-ele, ...), custom_call_target="tpu_custom_call" | custom-call | flops 7247757312 | bytes 41943040 | tf_op jit(solution)/shard_map/back_layer_1/pallas_call | solution.py:196
  163.7 54.0 %ffn_bwd.1 = (bf16[512,768]{1,0:T(8,128)(2,1)}, bf16[512,768]{1,0:T(8,128)(2,1)}, f32[512,768]{1,0:T(8,128)}, f32[8,768]{1,0:T(8,128)}, f32[8,3072]{1,0:T(8,128)...) custom-call(f32[512,768]{1,0:T(8,128)} %get-tuple-element.157.refs_0, ...), custom_call_target="tpu_custom_call" | custom-call | flops 10871635968 | bytes 41943040 | tf_op jit(solution)/shard_map/ffn_bwd/pallas_call | solution.py:196
  217.7 112.8 %back_layer_0.1 = (bf16[3,48,384]{2,1,0:T(8,128)(2,1)}, bf16[3,48,384]{2,1,0:T(8,128)(2,1)}, bf16[1,48,384]{2,1,0:T(8,128)(2,1)}, bf16[1,48,384]{2,1,0:T(8,128)(...) custom-call(bf16[2,12,256,512]{3,2,1,0:T(8,128)(2,1)} %get-tuple-ele, ...), custom_call_target="tpu_custom_call" | custom-call | flops 12079595520 | bytes 41943040 | tf_op jit(solution)/shard_map/back_layer_0/pallas_call | solution.py:196
  330.5 6.7 %finish.1 = (bf16[4,128,768]{2,1,0:T(8,128)(2,1)}, f32[4,256,768]{2,1,0:T(8,128)}, f32[2,3,48,768]{3,2,1,0:T(8,128)}, f32[2,48,768]{2,1,0:T(8,128)}, f32[2,48,76...) custom-call(bf16[2,48,128]{2,1,0:T(8,128)(2,1)} %get-tuple-element.1, ...), custom_call_target="tpu_custom_call" | custom-call | flops 1000000 | bytes 16777216 | tf_op jit(solution)/shard_map/finish/pallas_call | solution.py:196
  (5 shorter events, 0.0 us)
